TPU v7x, 32 devices: a whole 2x2x4 slice. The times are simulated.
32 devices in a mesh: ctx: 16 (over z, y, x), head: 2 (over core).
Axes of the slice: x: 2, y: 2, z: 4, core: 2. Of those that a mesh axis runs over, the one named last changes fastest.
Arguments:
- q_home: bfloat16 [8192, 2048], P('ctx', 'head'), may hold values from -18 to 18
- k_home: bfloat16 [8192, 512], P('ctx', 'head'), may hold values from -6 to 6
- value_slots_local: bfloat16 [8192, 512], P('ctx', 'head'), may hold values from -16 to 16
- out_weight: bfloat16 [2048, 4096], P('head'), may hold values from -0.125 to 0.125
- router: float32 [8192], P('ctx'), may hold values from 0.25 to 1
- positions: int32 [8192], P('ctx'), may hold values from 0 to 32767, as said below
- counts: int32 [16], P('ctx'), may hold values from 1 to 512, 2048 in all
Outputs:
- routed_update: bfloat16 [8192, 4096], P('ctx', 'head')
Inputs may be any that keep to these rules, and one draw needn't show every extreme that they name: counts sum to 2048; the busiest shard holds exactly 512. The 512 positions of shard d are distinct, increasing, and lie in [d * 2048, (d + 1) * 2048).
All inputs are finite; a program needn't handle non-finite values.
Results may differ from a plain program's by a relative error of at most 0.033.
Values may be sent and summed in bfloat16 or wider, within the bound.
A program may use at most 128 MiB of HBM per device.

v0:
```python
import functools

import jax
import jax.numpy as jnp
from jax import lax
from jax.experimental import pallas as pl
from jax.experimental.pallas import tpu as pltpu
from jax.sharding import PartitionSpec as P

HEAD_WIDTH = 128
PICKED_PER_SHARD = 128
QUERY_BLOCK = 128
TILE = 16
SWAP_PARTS = 4
LANES = 128
FAR = 1 << 28
LOW = -1e30

rope_theta = 500000.0


def inverse_freqs():
    half_dim = HEAD_WIDTH // 2
    return rope_theta ** (-(jnp.arange(half_dim, dtype=jnp.float32) * 2.0 / HEAD_WIDTH))


def angle_tables(positions):
    angles = positions.astype(jnp.float32)[:, None] * inverse_freqs()[None, :]
    cosine, sine = jnp.cos(angles), jnp.sin(angles)
    return cosine, sine


def rotate(rows, cosine, sine):
    half = HEAD_WIDTH // 2
    parts = []
    for at in range(0, rows.shape[1], HEAD_WIDTH):
        first = rows[:, at : at + half].astype(jnp.float32)
        second = rows[:, at + half : at + HEAD_WIDTH].astype(jnp.float32)
        parts.append(first * cosine - second * sine)
        parts.append(second * cosine + first * sine)
    return jnp.concatenate(parts, axis=1).astype(jnp.bfloat16)


def prefix_rows(x):
    rows = x.shape[0]
    row = lax.broadcasted_iota(jnp.int32, x.shape, 0)
    total = jnp.zeros_like(x)
    for e in range(rows - 1):
        total += jnp.where(row > e, x[e : e + 1, :], 0)
    return total


def arrange(shards):
    side = 1 << ((shards.bit_length() - 1) // 3)
    return shards // (side * side), side * side


def route(shards, packed, all_ref, cols, line_sem, plane_sem, relay_sem):
    lines, plane = arrange(shards)
    me = lax.axis_index("ctx")
    z, spot = me // plane, me % plane
    square = plane == 4
    direct = (1, 2) if square else tuple(range(1, plane))
    pieces = packed.shape[0]
    cut = pieces // 2
    halves = (pl.ds(0, cut), pl.ds(cut, pieces - cut))
    labels = [(0, 0)] + [(way, t) for t in range(1, lines) for way in (1, -1)]

    def valid(way, t):
        if way == 0:
            return True
        return z - t >= 0 if way == 1 else z + t < lines

    def when(way, t, body):
        if way == 0:
            body()
        else:
            pl.when(valid(way, t))(body)

    def line_of(way, t):
        return z - way * t

    def source(label):
        way, t = labels[label]
        if label == 0:
            return packed.at[:, :, cols]
        return all_ref.at[:, line_of(way, t) * plane + spot, :, cols]

    def hop(label, way):
        own_way, t = labels[label]
        arriving = labels.index((way, t + 1))
        target = line_of(own_way, t) * plane + spot
        return pltpu.make_async_remote_copy(
            src_ref=source(label),
            dst_ref=all_ref.at[:, target, :, cols],
            send_sem=line_sem.at[0, arriving],
            recv_sem=line_sem.at[1, arriving],
            device_id={"ctx": me + way * plane},
        )

    def hop_in(label):
        way, t = labels[label]
        here = all_ref.at[:, line_of(way, t) * plane + spot, :, cols]
        return pltpu.make_async_remote_copy(
            src_ref=here,
            dst_ref=here,
            send_sem=line_sem.at[0, label],
            recv_sem=line_sem.at[1, label],
            device_id={"ctx": me - way * plane},
        )

    def across(label, o):
        way, t = labels[label]
        return pltpu.make_async_remote_copy(
            src_ref=source(label),
            dst_ref=all_ref.at[:, line_of(way, t) * plane + spot, :, cols],
            send_sem=plane_sem.at[0, label, o],
            recv_sem=plane_sem.at[1, label, o],
            device_id={"ctx": z * plane + (spot ^ o)},
        )

    def across_in(label, o):
        way, t = labels[label]
        here = all_ref.at[:, line_of(way, t) * plane + (spot ^ o), :, cols]
        return pltpu.make_async_remote_copy(
            src_ref=here,
            dst_ref=here,
            send_sem=plane_sem.at[0, label, o],
            recv_sem=plane_sem.at[1, label, o],
            device_id={"ctx": z * plane + (spot ^ o)},
        )

    def relay(label, part, peer):
        way, t = labels[label]
        here = all_ref.at[halves[part], line_of(way, t) * plane + (spot ^ peer), :, cols]
        return pltpu.make_async_remote_copy(
            src_ref=here,
            dst_ref=here,
            send_sem=relay_sem.at[0, label, part],
            recv_sem=relay_sem.at[1, label, part],
            device_id={"ctx": z * plane + (spot ^ (3 - peer))},
        )

    def relay_in(label, part):
        way, t = labels[label]
        here = all_ref.at[halves[part], line_of(way, t) * plane + (spot ^ 3), :, cols]
        return pltpu.make_async_remote_copy(
            src_ref=here,
            dst_ref=here,
            send_sem=relay_sem.at[0, label, part],
            recv_sem=relay_sem.at[1, label, part],
            device_id={"ctx": z * plane + (spot ^ 3)},
        )

    def onward(label):
        way, t = labels[label]
        for next_way in (1, -1) if way == 0 else (way,):
            if t + 1 < lines:
                edge = z + 1 < lines if next_way == 1 else z - 1 >= 0
                yield next_way, edge

    def pass_on(label):
        for next_way, edge in onward(label):
            pl.when(edge)(hop(label, next_way).start)
        for o in direct:
            across(label, o).start()

    def relay_label(label):
        for part, peer in ((0, 1), (1, 2)):
            across_in(label, peer).wait_recv()
            if square:
                relay(label, part, peer).start()

    def relay_far(label):
        for o in direct:
            across_in(label, o).wait_recv()

    def finish(label):
        if square:
            for part, peer in ((0, 1), (1, 2)):
                relay_in(label, part).wait_recv()
                relay(label, part, peer).wait_send()
        for next_way, edge in onward(label):
            pl.when(edge)(hop(label, next_way).wait_send)
        for o in direct:
            across(label, o).wait_send()

    def arrive(label):
        hop_in(label).wait_recv()
        pass_on(label)

    take = relay_label if square else relay_far

    def each(body, steps):
        for label, (way, t) in enumerate(labels):
            if t in steps:
                when(way, t, functools.partial(body, label))

    return (
        functools.partial(pass_on, 0),
        lambda t: each(arrive, (t,)),
        lambda t: each(take, (t,)),
        lambda: each(finish, range(lines)),
    )


def spread_kernel(
    shards,
    kv_ref,
    cnt_ref,
    weight_ref,
    all_ref,
    cnt_all,
    swap_ref,
    recv,
    packed,
    send_sem,
    recv_sem,
    own_sem,
    swap_sem,
    line_sem,
    plane_sem,
    relay_sem,
):
    me = lax.axis_index("ctx")
    other = 1 - lax.axis_index("head")
    rows = kv_ref.shape[1]
    slots = shards * rows
    width = kv_ref.shape[2]
    pieces = packed.shape[0]
    shift = shards.bit_length() - 1
    peers = [lax.rem(me + o, shards) for o in range(shards)]

    barrier = pltpu.get_barrier_semaphore()
    for o in range(1, shards):
        pl.semaphore_signal(barrier, inc=1, device_id={"ctx": peers[o]})
    pl.semaphore_signal(barrier, inc=1, device_id={"head": other})
    own_kv = pltpu.make_async_copy(kv_ref.at[0], recv.at[me], own_sem.at[0])
    own_kv.start()
    own_cnt = pltpu.make_async_copy(cnt_ref, cnt_all.at[me], own_sem.at[1])
    own_cnt.start()
    pl.semaphore_wait(barrier, shards)

    def remote(kind, o, src, dst):
        return pltpu.make_async_remote_copy(
            src_ref=src,
            dst_ref=dst,
            send_sem=send_sem.at[kind, o],
            recv_sem=recv_sem.at[kind, o],
            device_id={"ctx": peers[o]},
        )

    cnt_copies = [remote(0, o, cnt_ref, cnt_all.at[me]) for o in range(1, shards)]
    half_width = width // 2
    columns_of = [pl.ds(i * half_width, half_width) for i in range(2)]
    kv_copies = [
        [
            remote(1 + i, o, kv_ref.at[o, :, cols], recv.at[me, :, cols])
            for o in range(1, shards)
        ]
        for i, cols in enumerate(columns_of)
    ]
    for c in cnt_copies:
        c.start()
    for c in kv_copies[0] + kv_copies[1]:
        c.start()
    depth = weight_ref.shape[0] // SWAP_PARTS
    half = swap_ref.shape[1]
    columns = pl.ds(pl.multiple_of(other * half, half), half)
    swaps = []
    for i in range(SWAP_PARTS):
        at = pl.ds(i * depth, depth)
        swaps.append(
            pltpu.make_async_remote_copy(
                src_ref=weight_ref.at[at, columns],
                dst_ref=swap_ref.at[at, :],
                send_sem=swap_sem.at[0, i],
                recv_sem=swap_sem.at[1, i],
                device_id={"head": other},
            )
        )
    for c in swaps:
        c.start()
    own_kv.wait()
    own_cnt.wait()
    for c in cnt_copies:
        c.wait()
    counts = cnt_all[:, 0, :]
    source = lax.broadcasted_iota(jnp.int32, counts.shape, 0)
    lead = (me - source + shards) & (shards - 1)
    taken = (counts + (shards - 1) - lead) >> shift
    start = prefix_rows(taken)
    wide = (shards, slots)
    taken_w = jnp.broadcast_to(taken[:, :1], wide)
    start_w = jnp.broadcast_to(start[:, :1], wide)
    within = lax.broadcasted_iota(jnp.int32, wide, 1) - rows * lax.broadcasted_iota(
        jnp.int32, wide, 0
    )
    live = (within >= 0) & (within < taken_w)
    target = jnp.sum(jnp.where(live, start_w + within + 1, 0), axis=0, keepdims=True) - 1
    place = lax.broadcasted_iota(jnp.int32, (pieces * TILE, slots), 0)
    pick = jnp.where(place == target, 1.0, 0.0).astype(jnp.bfloat16)
    routes, own_pieces = [], []
    for i, cols in enumerate(columns_of):
        for c in kv_copies[i]:
            c.wait()
        got = recv[:, :, cols].reshape(slots, half_width)
        packed[:, :, cols] = (
            jnp.dot(pick, got, preferred_element_type=jnp.float32)
            .astype(jnp.bfloat16)
            .reshape(packed.shape[0], TILE, half_width)
        )
        routes.append(
            route(
                shards, packed, all_ref, cols, line_sem.at[i], plane_sem.at[i], relay_sem.at[i]
            )
        )
        routes[i][0]()
        own_pieces.append(
            pltpu.make_async_copy(
                packed.at[:, :, cols], all_ref.at[:, me, :, cols], own_sem.at[2 + i]
            )
        )
        own_pieces[i].start()
    lines = arrange(shards)[0]
    for t in range(1, lines):
        for _, arrive, _, _ in routes:
            arrive(t)
        for _, _, take, _ in routes:
            take(t - 1)
    for _, _, take, _ in routes:
        take(lines - 1)
    for _, _, _, finish in routes:
        finish()
    for c in own_pieces:
        c.wait()
    for c in swaps:
        c.wait()


def spread(kv_send, counts, weight, shards, pieces):
    rows, width = kv_send.shape[1:]
    lines, plane = arrange(shards)
    return pl.pallas_call(
        functools.partial(spread_kernel, shards),
        out_shape=(
            jax.ShapeDtypeStruct((pieces, shards, TILE, width), jnp.bfloat16),
            jax.ShapeDtypeStruct((shards, 8, LANES), jnp.int32),
            jax.ShapeDtypeStruct((weight.shape[0], weight.shape[1] // 2), weight.dtype),
        ),
        in_specs=[pl.BlockSpec(memory_space=pltpu.VMEM)] * 2
        + [pl.BlockSpec(memory_space=pl.ANY)],
        out_specs=(
            pl.BlockSpec(memory_space=pl.ANY),
            pl.BlockSpec(memory_space=pltpu.VMEM),
            pl.BlockSpec(memory_space=pl.ANY),
        ),
        scratch_shapes=[
            pltpu.VMEM((shards, rows, width), jnp.bfloat16),
            pltpu.VMEM((pieces, TILE, width), jnp.bfloat16),
            pltpu.SemaphoreType.DMA((3, shards)),
            pltpu.SemaphoreType.DMA((3, shards)),
            pltpu.SemaphoreType.DMA((4,)),
            pltpu.SemaphoreType.DMA((2, SWAP_PARTS)),
            pltpu.SemaphoreType.DMA((2, 2, 2 * lines - 1)),
            pltpu.SemaphoreType.DMA((2, 2, 2 * lines - 1, plane)),
            pltpu.SemaphoreType.DMA((2, 2, 2 * lines - 1, 2)),
        ],
        compiler_params=pltpu.CompilerParams(collective_id=0, has_side_effects=True),
        name="spread",
    )(kv_send, counts, weight)


def attend_kernel(
    shards,
    chunks,
    q_ref,
    cos_ref,
    sin_ref,
    cnt_ref,
    kv_ref,
    out_ref,
    q_s,
    top_s,
    sum_s,
    acc_s,
    table_s,
    name_s,
):
    me = lax.axis_index("ctx")
    step = pl.program_id(0)
    blocks, groups, stack, _ = q_s.shape
    share = stack // QUERY_BLOCK
    keys = kv_ref.shape[0] // chunks
    shift = shards.bit_length() - 1
    factor = 1.4426950408889634 / HEAD_WIDTH**0.5

    counts = cnt_ref[:, 0, :]
    shard_row = lax.broadcasted_iota(jnp.int32, counts.shape, 0)
    own_start = jnp.sum(jnp.where(shard_row < me, counts, 0)[:, :1])
    own_count = jnp.sum(jnp.where(shard_row == me, counts, 0)[:, :1])
    live_blocks = (own_count + (QUERY_BLOCK - 1)) >> (QUERY_BLOCK.bit_length() - 1)
    grid_shape = (keys, LANES)
    key_row = lax.broadcasted_iota(jnp.int32, grid_shape, 0)

    @pl.when(step == 0)
    def _():
        lane = lax.broadcasted_iota(jnp.int32, counts.shape, 1)
        count_row = jnp.sum(jnp.where(shard_row == lane, counts, 0), axis=0, keepdims=True)
        offset_row = jnp.sum(jnp.where(shard_row < lane, counts, 0), axis=0, keepdims=True)
        source = lax.broadcasted_iota(jnp.int32, grid_shape, 1)
        lead = ((key_row >> 4) - source) & (shards - 1)
        taken = jnp.where(source < shards, (count_row + (shards - 1) - lead) >> shift, 0)
        earlier = (
            lax.broadcasted_iota(jnp.int32, (LANES, LANES), 0)
            < lax.broadcasted_iota(jnp.int32, (LANES, LANES), 1)
        )
        start = jnp.dot(
            taken.astype(jnp.float32).astype(jnp.bfloat16),
            jnp.where(earlier, 1.0, 0.0).astype(jnp.bfloat16),
            preferred_element_type=jnp.float32,
        ).astype(jnp.int32)
        table_s[0] = (key_row & (TILE - 1)) - start
        table_s[1] = taken
        table_s[2] = offset_row + lead

        @pl.loop(0, live_blocks)
        def _(b):
            top_s[b] = jnp.full_like(top_s[b], LOW)
            sum_s[b] = jnp.zeros_like(sum_s[b])
            acc_s[b] = jnp.zeros_like(acc_s[b])
            at = pl.ds(pl.multiple_of(b * QUERY_BLOCK, QUERY_BLOCK), QUERY_BLOCK)
            cosine, sine = cos_ref[at, :], sin_ref[at, :]
            for g in range(groups):
                for h in range(share):
                    cols = pl.ds((g * share + h) * HEAD_WIDTH, HEAD_WIDTH)
                    x = q_ref[at, cols].astype(jnp.float32)
                    turned = x * cosine + pltpu.roll(x, HEAD_WIDTH // 2, 1) * sine
                    q_s[b, g, pl.ds(h * QUERY_BLOCK, QUERY_BLOCK), :] = turned.astype(jnp.bfloat16)

    firsts, last_name = [], None
    for j in range(chunks):
        within = table_s[0] + (step * chunks + j) * TILE
        held = (within >= 0) & (within < table_s[1])
        names = jnp.min(
            jnp.where(held, table_s[2] + (within << shift), FAR), axis=1, keepdims=True
        )
        name_s[pl.ds(j * keys, keys), :] = names
        firsts.append(jnp.min(names))
        last = jnp.max(names)
        last_name = last if last_name is None else jnp.maximum(last_name, last)

    def update(b, first_query, used, masked):
        rows = pl.ds(0, used * keys)
        scores = []
        for g in range(groups):
            key = kv_ref[rows, pl.ds(g * HEAD_WIDTH, HEAD_WIDTH)]
            scores.append(
                lax.dot_general(
                    key, q_s[b, g], (((1,), (1,)), ((), ())), preferred_element_type=jnp.float32
                )
            )
        if masked:
            query = first_query + lax.broadcasted_iota(
                jnp.int32, (used * keys, QUERY_BLOCK), 1
            )
            bias = jnp.where(name_s[rows, :] <= query, 0.0, LOW)
            bias = jnp.concatenate([bias] * share, axis=1)
            scores = [x + bias for x in scores]
        for g in range(groups):
            value = kv_ref[rows, pl.ds((groups + g) * HEAD_WIDTH, HEAD_WIDTH)]
            old = top_s[b, g]
            top = jnp.maximum(old, jnp.max(scores[g], axis=0, keepdims=True))
            terms = jnp.exp2((scores[g] - top) * factor)
            rescale = jnp.exp2((old - top) * factor)
            top_s[b, g] = top
            sum_s[b, g] = sum_s[b, g] * rescale + jnp.sum(terms, axis=0, keepdims=True)
            acc_s[b, g] = acc_s[b, g] * rescale + lax.dot_general(
                value,
                terms.astype(jnp.bfloat16),
                (((0,), (0,)), ((), ())),
                preferred_element_type=jnp.float32,
            )

    @pl.loop(0, live_blocks)
    def _(b):
        first_query = own_start + b * QUERY_BLOCK
        needed = sum((f < first_query + QUERY_BLOCK).astype(jnp.int32) for f in firsts)
        plain = last_name <= first_query
        for used in range(1, chunks + 1):
            chosen = needed == used
            if used == chunks:
                pl.when(plain)(functools.partial(update, b, first_query, used, False))
                chosen = chosen & jnp.logical_not(plain)
            pl.when(chosen)(functools.partial(update, b, first_query, used, True))

    @pl.when(step == pl.num_programs(0) - 1)
    def _():
        for b in range(blocks):
            at = pl.ds(b * QUERY_BLOCK, QUERY_BLOCK)

            @pl.when(b < live_blocks)
            def _():
                for g in range(groups):
                    done = acc_s[b, g] / sum_s[b, g]
                    for h in range(share):
                        part = done[:, h * QUERY_BLOCK : (h + 1) * QUERY_BLOCK]
                        out_ref[at, pl.ds((g * share + h) * HEAD_WIDTH, HEAD_WIDTH)] = (
                            part.T.astype(jnp.bfloat16)
                        )

            @pl.when(b >= live_blocks)
            def _():
                out_ref[at, :] = jnp.zeros((QUERY_BLOCK, out_ref.shape[1]), jnp.bfloat16)


def attend(q_home, cosine, sine, cnt_all, kv_all, shards):
    slots, features = q_home.shape
    pieces, keys, width = kv_all.shape
    chunks = 3 if pieces % 3 == 0 and shards <= 32 else 1
    kv_all = kv_all.reshape(pieces * keys, width)
    groups = width // (2 * HEAD_WIDTH)
    share = features // HEAD_WIDTH // groups
    blocks = slots // QUERY_BLOCK
    stack = share * QUERY_BLOCK
    whole = lambda a: pl.BlockSpec(a.shape, lambda i: (0,) * a.ndim)
    return pl.pallas_call(
        functools.partial(attend_kernel, shards, chunks),
        out_shape=jax.ShapeDtypeStruct((slots, features), jnp.bfloat16),
        grid=(pieces // chunks,),
        in_specs=[
            whole(q_home),
            whole(cosine),
            whole(sine),
            whole(cnt_all),
            pl.BlockSpec((chunks * keys, width), lambda i: (i, 0)),
        ],
        out_specs=pl.BlockSpec((slots, features), lambda i: (0, 0)),
        scratch_shapes=[
            pltpu.VMEM((blocks, groups, stack, HEAD_WIDTH), jnp.bfloat16),
            pltpu.VMEM((blocks, groups, 1, stack), jnp.float32),
            pltpu.VMEM((blocks, groups, 1, stack), jnp.float32),
            pltpu.VMEM((blocks, groups, HEAD_WIDTH, stack), jnp.float32),
            pltpu.VMEM((3, keys, LANES), jnp.int32),
            pltpu.VMEM((chunks * keys, 1), jnp.int32),
        ],
        name="attend",
    )(q_home, cosine, sine, cnt_all, kv_all)


def trade_kernel(mine_ref, theirs_ref, sems):
    other = 1 - lax.axis_index("head")
    barrier = pltpu.get_barrier_semaphore()
    pl.semaphore_signal(barrier, inc=1, device_id={"head": other})
    pl.semaphore_wait(barrier, 1)
    depth = mine_ref.shape[0] // SWAP_PARTS
    copies = []
    for i in range(SWAP_PARTS):
        at = pl.ds(i * depth, depth)
        copies.append(
            pltpu.make_async_remote_copy(
                src_ref=mine_ref.at[at, :],
                dst_ref=theirs_ref.at[at, :],
                send_sem=sems.at[0, i],
                recv_sem=sems.at[1, i],
                device_id={"head": other},
            )
        )
    for c in copies:
        c.start()
    for c in copies:
        c.wait()


def trade(mine):
    return pl.pallas_call(
        trade_kernel,
        out_shape=jax.ShapeDtypeStruct(mine.shape, mine.dtype),
        in_specs=[pl.BlockSpec(memory_space=pl.ANY)],
        out_specs=pl.BlockSpec(memory_space=pl.ANY),
        scratch_shapes=[pltpu.SemaphoreType.DMA((2, SWAP_PARTS))],
        compiler_params=pltpu.CompilerParams(collective_id=1, has_side_effects=True),
        name="trade",
    )(mine)


def project_kernel(head_ref, count_ref, mine_ref, theirs_ref, own_w, got_w, router_ref, out_ref):
    blocks = mine_ref.shape[0] // QUERY_BLOCK
    count = count_ref[0]
    square = (QUERY_BLOCK, QUERY_BLOCK)
    row = lax.broadcasted_iota(jnp.int32, square, 0)
    diagonal = row == lax.broadcasted_iota(jnp.int32, square, 1)
    for b in range(blocks):
        at = pl.ds(b * QUERY_BLOCK, QUERY_BLOCK)

        @pl.when(b * QUERY_BLOCK < count)
        def _():
            summed = jnp.dot(mine_ref[at, :], own_w[...], preferred_element_type=jnp.float32)
            summed += jnp.dot(theirs_ref[at, :], got_w[...], preferred_element_type=jnp.float32)
            summed = summed.astype(jnp.bfloat16).astype(jnp.float32)
            gain = jnp.sum(
                jnp.where(diagonal, router_ref[b : b + 1, :], 0.0), axis=1, keepdims=True
            )
            live = b * QUERY_BLOCK + row[:, :1] < count
            out_ref[at, :] = jnp.where(live, gain * summed, 0.0).astype(jnp.bfloat16)

        @pl.when(b * QUERY_BLOCK >= count)
        def _():
            out_ref[at, :] = jnp.zeros((QUERY_BLOCK, out_ref.shape[1]), jnp.bfloat16)


def project(head, counts, mine, theirs, weight, swapped, router):
    slots, features = mine.shape
    half = swapped.shape[1]
    tile = min(512, half)
    tiles = half // tile
    gains = router.reshape(slots // QUERY_BLOCK, QUERY_BLOCK)
    whole = lambda a: pl.BlockSpec(a.shape, lambda i, h, c: (0,) * a.ndim)
    return pl.pallas_call(
        project_kernel,
        out_shape=jax.ShapeDtypeStruct((slots, half), jnp.bfloat16),
        grid_spec=pltpu.PrefetchScalarGridSpec(
            num_scalar_prefetch=2,
            grid=(tiles,),
            in_specs=[
                whole(mine),
                whole(theirs),
                pl.BlockSpec((features, tile), lambda i, h, c: (0, h[0] * tiles + i)),
                pl.BlockSpec((features, tile), lambda i, h, c: (0, i)),
                whole(gains),
            ],
            out_specs=pl.BlockSpec((slots, tile), lambda i, h, c: (0, i)),
        ),
        name="project",
    )(head, counts, mine, theirs, weight, swapped, gains)


def local(q_home, k_home, value_slots_local, out_weight, router, positions, counts):
    shards = lax.axis_size("ctx")
    slot_count = q_home.shape[0]
    peer_rows = slot_count // shards
    cap = PICKED_PER_SHARD + (shards - 1) // 2
    pieces = -(-cap // TILE)
    cosine, sine = angle_tables(positions)
    wide_cosine = jnp.concatenate([cosine, cosine], axis=1)
    wide_sine = jnp.concatenate([-sine, sine], axis=1)
    kv = jnp.concatenate([rotate(k_home, cosine, sine), value_slots_local], axis=1)
    width = kv.shape[1]
    kv_send = kv.reshape(peer_rows, shards, width).transpose(1, 0, 2)
    short = max(0, TILE - peer_rows)
    kv_send = jnp.pad(kv_send, ((0, 0), (0, short), (0, 0)))
    own = jnp.broadcast_to(counts[:, None], (8, LANES))
    kv_all, cnt_all, swapped = spread(kv_send, own, out_weight, shards, pieces)
    kv_all = kv_all.reshape(pieces, shards * TILE, width)
    attended = attend(q_home, wide_cosine, wide_sine, cnt_all, kv_all, shards)
    theirs = trade(attended)
    head = lax.axis_index("head").astype(jnp.int32).reshape(1)
    return project(head, counts, attended, theirs, out_weight, swapped, router)


def solution(mesh):
    return jax.shard_map(
        local,
        mesh=mesh,
        in_specs=(
            P("ctx", "head"),
            P("ctx", "head"),
            P("ctx", "head"),
            P("head", None),
            P("ctx"),
            P("ctx"),
            P("ctx"),
        ),
        out_specs=P("ctx", "head"),
        check_vma=False,
    )
```

profile of v0, /device:TPU:23, one launch (start us, length us, event | category | flops | bytes accessed | tf_op | source)
XLA Modules:
  0.0 82.0 jit_solution(9200124317301989269)
XLA Ops:
  0.7 0.7 convert_element_type.16
  1.4 0.6 broadcast_in_dim.5.cnt_ref
  1.9 2.2 %fusion.16 = (bf16[512,64]{1,0:T(8,128)(2,1)S(1)}, bf16[512,64]{1,0:T(8,128)(2,1)S(1)}, bf16[512,64]{1,0:T(8,128)(2,1)S(1)}, bf16[512,64]{1,0:T(8,128)(2,1)S(1)}...) fusion(f32[512]{0:T(512)S(1)} %convert_element_type.16, f32[64]{0:T(128)S(1)} %negate_power_fusion, ...), kind=kLoop, calls=%fused_computation.19 | loop fusion | flops 720896 | bytes 919808 | tf_op jit(solution)/shard_map/convert.3
  4.2 1.2 %concatenate.14 = bf16[512,512]{1,0:T(8,128)(2,1)S(1)} concatenate(bf16[512,64]{1,0:T(8,128)(2,1)S(1)} %get-tuple-element.14, bf16[512,64]{1,0:T(8,128)(2,1)S(1)} %get-tuple-element.13, bf16[512,64]{1,0:T(8,128)(2,1)S(1)} %get-tuple-element.12, bf16[512,64]{1,0:T(8,128)(2,1)S(1)} %get-tuple-element.11, bf16[512,256]{1,0:T(8,128)(2,1)} %param.9), dimensions={1} | concatenate | bytes 1048576 | tf_op jit(solution)/shard_map/concatenate | solution.py:647
  5.4 1.1 %copy.12 = bf16[32,16,512]{2,0,1:T(8,128)(2,1)} copy(bf16[32,16,512]{2,1,0:T(8,128)(2,1)S(1)} %bitcast.11) | data formatting | bytes 1048576 | tf_op jit(solution)/shard_map/reshape | solution.py:649
  6.5 1.0 %pad_maximum_fusion = (f32[512,128]{1,0:T(8,128)}, f32[512,128]{1,0:T(8,128)}) fusion(f32[512,64]{1,0:T(8,128)S(1)} %get-tuple-element.17, f32[512,64]{1,0:T(8,128)S(1)} %get-tuple-element.15, f32[512,64]{1,0:T(8,128)S(1)} %get-tuple-element.16), kind=kLoop, calls=%fused_computation.20 | loop fusion | flops 131072 | bytes 917504 | tf_op jit(solution)/shard_map/concatenate | solution.py:645
  7.5 41.0 %spread.1 = (bf16[9,16,16,512]{3,2,1,0:T(8,128)(2,1)}, s32[16,8,128]{2,1,0:T(8,128)}, bf16[1024,2048]{1,0:T(8,128)(2,1)}) custom-call(bf16[16,32,512]{2,1,0:T(8,128)(2,1)} %bitcast.10, s32[8,128]{1,0:T(8,128)} %broadcast_in_dim.5.cnt_ref, bf16[1024,4096]{1,0:T(8,128)(2,1)} %own_w.1), custom_call_target="tpu_custom_call" | custom-call | tf_op jit(solution)/shard_map/spread/pallas_call | solution.py:344
  48.5 19.3 %attend.1.mine_ref = bf16[512,1024]{1,0:T(8,128)(2,1)} custom-call(bf16[512,1024]{1,0:T(8,128)(2,1)} %q_ref.1, f32[512,128]{1,0:T(8,128)} %get-tuple-element.18.cos_ref, f32[512,128]{1,0:T(8,128)} %get-tuple-element.19.sin_ref, s32[16,8,128]{2,1,0:T(8,128)} %get-tuple-element.8.cnt_ref, bf16[2304,512]{1,0:T(8,128)(2,1)} %bitcast.9), custom_call_target="tpu_custom_call" | custom-call | tf_op jit(solution)/shard_map/attend/pallas_call | solution.py:527
  67.8 3.8 %trade.1.theirs_ref = bf16[512,1024]{1,0:T(8,128)(2,1)} custom-call(bf16[512,1024]{1,0:T(8,128)(2,1)} %attend.1.mine_ref), custom_call_target="tpu_custom_call" | custom-call | tf_op jit(solution)/shard_map/trade/pallas_call | solution.py:576
  71.6 10.5 %project.1 = bf16[512,2048]{1,0:T(8,128)(2,1)} custom-call(s32[1]{0:T(128)} %bitcast.head_ref, s32[1]{0:T(128)} %copy.13.count_ref, bf16[512,1024]{1,0:T(8,128)(2,1)} %attend.1.mine_ref, bf16[512,1024]{1,0:T(8,128)(2,1)} %trade.1.theirs_ref, bf16[1024,4096]{1,0:T(8,128)(2,1)} %own_w.1, bf16[1024,2048]{1,0:T(8,128)(2,1)} %get-tuple-element.10.got_w, ...), custom_call_target="tpu_custom_call" | custom-call | tf_op jit(solution)/shard_map/project/pallas_call | solution.py:619
  (1 shorter events, 0.0 us)
where the time goes:
time: 82.3 us; the launch traced here: 82 us
  Pallas kernels  74.5 us (91%)
  other arithmetic  3.95 us (5%)
  local copies, waits for them, and re-layouts  2.88 us (3%)
    pallas_call x1, Pallas kernels, spread(): pl.pallas_call(functools.partial(spread_kernel, shards), out_shape=(jax.S...  41 us
    pallas_call x1, Pallas kernels, attend(): pl.pallas_call(functools.partial(attend_kernel, shards, chunks), out_shap...  19.3 us
    pallas_call x1, Pallas kernels, project(): pl.pallas_call(project_kernel, out_shape=jax.ShapeDtypeStruct((slots, hal...  10.5 us
    pallas_call x1, Pallas kernels, trade(): pl.pallas_call(trade_kernel, out_shape=jax.ShapeDtypeStruct(mine.shape, m...  3.75 us
    another operation x1, other arithmetic  2.24 us

commit v1 on v0

v1 whole, which is shorter than its diff:
```python
import functools
import math

import jax
import jax.numpy as jnp
from jax import lax
from jax.experimental import pallas as pl
from jax.experimental.pallas import tpu as pltpu
from jax.sharding import PartitionSpec as P

HEAD_WIDTH = 128
PICKED_PER_SHARD = 128
QUERY_BLOCK = 128
TILE = 16
SWAP_PARTS = 4
LANES = 128
COLUMN_TILE = 512
SPAN = 4
FAR = 1 << 28
LOW = -1e30
QUARTER = 1 << 30
SINE_TERMS = (
    6.283185159611168,
    -41.34165492934356,
    81.60099819261757,
    -76.54965682073457,
    39.53581371237487,
)

rope_theta = 500000.0


def turns_per_position():
    half = HEAD_WIDTH // 2
    turns = [rope_theta ** (-2.0 * i / HEAD_WIDTH) / (2.0 * math.pi) for i in range(half)]
    return [round(t * 4294967296.0) for t in turns]


def cosine_of(phase):
    fold = 0.25 - jnp.abs(phase.astype(jnp.float32) * (1.0 / 4294967296.0))
    square = fold * fold
    total = jnp.full_like(square, SINE_TERMS[-1])
    for term in SINE_TERMS[-2::-1]:
        total = total * square + term
    return total * fold


def turn(x, cosine, sine):
    return x * cosine + pltpu.roll(x, HEAD_WIDTH // 2, 1) * sine


def as_column(row):
    square = jnp.broadcast_to(row, (LANES, LANES))
    return square.T


def arrange(shards):
    side = 1 << ((shards.bit_length() - 1) // 3)
    return shards // (side * side), side * side


def plan(shards):
    lines, plane = arrange(shards)
    most = PICKED_PER_SHARD * lines + lines * (plane - 1) // 2
    room = -(-most // TILE) * TILE
    step = 96 if plane == 4 else 128
    sizes = [room % step] if room % step else []
    sizes += [step] * (room // step)
    return tuple(sizes)


def fused_kernel(
    shards,
    sizes,
    count_ref,
    pos_ref,
    router_ref,
    q_ref,
    k_ref,
    v_ref,
    weight_ref,
    out_ref,
    kin,
    q_in,
    pos_s,
    router_s,
    cos_s,
    sin_s,
    send,
    recv,
    inbox,
    kv,
    cnt_all,
    name_s,
    q_s,
    top_s,
    sum_s,
    acc_s,
    gain_s,
    own_w,
    got_w,
    mine_s,
    theirs_s,
    part_s,
    out_s,
    load_sem,
    cnt_sem,
    up_cnt_sem,
    deal_sem,
    up_sem,
    plane_sem,
    relay_sem,
    swap_sem,
    trade_sem,
    out_sem,
):
    lines, plane = arrange(shards)
    shift = plane.bit_length() - 1
    me = lax.axis_index("ctx")
    head = lax.axis_index("head")
    other = 1 - head
    z, spot = me // plane, me % plane
    square = plane == 4
    direct = (1, 2) if square else tuple(range(1, plane))
    pieces, _, deep, width = send.shape
    slots = q_in.shape[0]
    span = pieces * plane * deep
    blocks, groups, stack, _ = q_s.shape
    share = stack // QUERY_BLOCK
    keyed = k_ref.shape[1]
    half = own_w.shape[1]
    steps = len(sizes)
    firsts = [sum(sizes[:i]) for i in range(steps)]
    room = sum(sizes)
    factor = 1.4426950408889634 / HEAD_WIDTH**0.5

    count = count_ref[0]
    cnt_all[...] = jnp.zeros_like(cnt_all)
    cnt_all[me] = jnp.full(cnt_all.shape[1:], count, jnp.int32)

    barrier = pltpu.get_barrier_semaphore()
    for o in range(1, plane):
        pl.semaphore_signal(barrier, inc=1, device_id={"ctx": z * plane + (spot ^ o)})
    pl.semaphore_signal(barrier, inc=1, device_id={"head": other})

    @pl.when(z + 1 < lines)
    def _():
        pl.semaphore_signal(barrier, inc=1, device_id={"ctx": me + plane})

    @pl.when(z > 0)
    def _():
        pl.semaphore_signal(barrier, inc=1, device_id={"ctx": me - plane})

    loads = [
        pltpu.make_async_copy(pos_ref, pos_s, load_sem.at[0]),
        pltpu.make_async_copy(k_ref, kin.at[:, pl.ds(0, keyed)], load_sem.at[1]),
        pltpu.make_async_copy(v_ref, kin.at[:, pl.ds(keyed, keyed)], load_sem.at[2]),
        pltpu.make_async_copy(q_ref, q_in, load_sem.at[3]),
        pltpu.make_async_copy(router_ref, router_s, load_sem.at[4]),
        pltpu.make_async_copy(
            weight_ref.at[:, pl.ds(pl.multiple_of(head * half, half), half)],
            own_w,
            load_sem.at[5],
        ),
    ]
    for c in loads[:5]:
        c.start()

    lane = lax.broadcasted_iota(jnp.int32, (1, LANES), 1)
    rate = jnp.zeros((1, LANES), jnp.int32)
    for i, value in enumerate(turns_per_position()):
        rate = jnp.where((lane & (HEAD_WIDTH // 2 - 1)) == i, value, rate)
    lead = jnp.where(lane < HEAD_WIDTH // 2, QUARTER, -QUARTER)
    loads[0].wait()
    for b in range(blocks):
        at = pl.ds(b * QUERY_BLOCK, QUERY_BLOCK)
        column = as_column(pos_s[b : b + 1, :].astype(jnp.float32)).astype(jnp.int32)
        phase = column * rate
        cos_s[at, :] = cosine_of(phase)
        sin_s[at, :] = cosine_of(phase + lead)

    loads[1].wait()
    loads[2].wait()
    block = plane * deep
    row = lax.broadcasted_iota(jnp.int32, (block, block), 0)
    column = lax.broadcasted_iota(jnp.int32, (block, block), 1)
    chosen = column == plane * (row % deep) + row // deep
    deal_map = jnp.where(chosen, 1.0, 0.0).astype(jnp.bfloat16)
    for t in range(pieces):
        at = pl.ds(t * block, block)
        parts = []
        for c in range(keyed // HEAD_WIDTH):
            x = kin[at, pl.ds(c * HEAD_WIDTH, HEAD_WIDTH)].astype(jnp.float32)
            parts.append(turn(x, cos_s[at, :], sin_s[at, :]).astype(jnp.bfloat16))
        parts.append(kin[at, pl.ds(keyed, keyed)])
        rows = jnp.concatenate(parts, axis=1)
        dealt = jnp.dot(deal_map, rows, preferred_element_type=jnp.float32)
        send[t] = dealt.astype(jnp.bfloat16).reshape(plane, deep, width)

    greeted = plane + (z > 0).astype(jnp.int32) + (z + 1 < lines).astype(jnp.int32)
    pl.semaphore_wait(barrier, greeted)

    def mate(o):
        return {"ctx": z * plane + ((spot + o) & (plane - 1))}

    def remote(src, dst, sems, index, target):
        return pltpu.make_async_remote_copy(
            src_ref=src,
            dst_ref=dst,
            send_sem=sems.at[(0,) + index],
            recv_sem=sems.at[(1,) + index],
            device_id=target,
        )

    cnt_copies = [
        remote(cnt_all.at[me], cnt_all.at[me], cnt_sem, (o,), mate(o)) for o in range(1, plane)
    ]
    for c in cnt_copies:
        c.start()
    deals = [
        [
            remote(send.at[t, o], recv.at[t, spot], deal_sem, (t, o), mate(o))
            for o in range(1, plane)
        ]
        for t in range(pieces)
    ]
    for piece in deals:
        for c in piece:
            c.start()
    for t in range(pieces):
        recv[t, spot] = send[t, 0]
    depth = weight_ref.shape[0] // SWAP_PARTS
    columns = pl.ds(pl.multiple_of(other * half, half), half)
    swaps = []
    for i in range(SWAP_PARTS):
        at = pl.ds(i * depth, depth)
        swaps.append(
            remote(
                weight_ref.at[at, columns], got_w.at[at, :], swap_sem, (i,), {"head": other}
            )
        )
    for c in swaps:
        c.start()
    loads[5].start()

    loads[3].wait()

    @pl.loop(0, blocks)
    def _(b):
        top_s[b] = jnp.full_like(top_s[b], LOW)
        sum_s[b] = jnp.zeros_like(sum_s[b])
        acc_s[b] = jnp.zeros_like(acc_s[b])
        at = pl.ds(pl.multiple_of(b * QUERY_BLOCK, QUERY_BLOCK), QUERY_BLOCK)
        cosine, sine = cos_s[at, :] * factor, sin_s[at, :] * factor
        for g in range(groups):
            for h in range(share):
                x = q_in[at, pl.ds((g * share + h) * HEAD_WIDTH, HEAD_WIDTH)].astype(jnp.float32)
                q_s[b, g, pl.ds(h * QUERY_BLOCK, QUERY_BLOCK), :] = turn(x, cosine, sine).astype(
                    jnp.bfloat16
                )

    def table_rows(p):
        return cnt_all.at[pl.ds(p * plane, plane)]

    def up_counts(far):
        rows = table_rows(z - far)
        return remote(rows, rows, up_cnt_sem, (far + 1,), {"ctx": me + plane})

    def up_counts_in(far):
        rows = table_rows(z - far)
        return remote(rows, rows, up_cnt_sem, (far,), {"ctx": me - plane})

    for c in cnt_copies:
        c.wait_recv()
    pl.when(z + 1 < lines)(lambda: up_counts(0).start())
    for far in range(1, lines):

        @pl.when(z >= far)
        def _():
            up_counts_in(far).wait_recv()
            if far + 1 < lines:
                pl.when(z + 1 < lines)(lambda: up_counts(far).start())

    def dealt_to(line, counts, source):
        skip = (line - source) & (plane - 1)
        return (counts + (plane - 1) - skip) >> shift, skip

    counts = cnt_all[:, 0, :]
    shard_row = lax.broadcasted_iota(jnp.int32, counts.shape, 0)
    held, _ = dealt_to(spot, counts, shard_row)
    below = jnp.sum(jnp.where(shard_row < z * plane, held, 0), axis=0, keepdims=True)
    segments = pieces * plane
    seg = lax.broadcasted_iota(jnp.int32, (segments, LANES), 0)
    seg_held = jnp.zeros((segments, LANES), jnp.int32)
    for s in range(plane):
        mine = jnp.broadcast_to(cnt_all[z * plane + s, 0:1, :], seg.shape)
        seg_held = jnp.where((seg & (plane - 1)) == s, mine, seg_held)
    seg_held, _ = dealt_to(spot, seg_held, seg)
    seg_held = jnp.clip(seg_held - deep * (seg >> shift), 0, deep)
    seg_start = jnp.broadcast_to(below, seg.shape)
    for e in range(segments - 1):
        seg_start += jnp.where(seg > e, seg_held[e : e + 1, :], 0)
    wide = (segments, span)
    wide_held = jnp.broadcast_to(seg_held[:, :1], wide)
    wide_start = jnp.broadcast_to(seg_start[:, :1], wide)
    within = lax.broadcasted_iota(jnp.int32, wide, 1) - deep * lax.broadcasted_iota(
        jnp.int32, wide, 0
    )
    live = (within >= 0) & (within < wide_held)
    target = jnp.sum(jnp.where(live, wide_start + within + 1, 0), axis=0, keepdims=True) - 1

    arrived = [0]

    def region(k, line):
        start = plane * firsts[k] + line * sizes[k]
        return pl.ds(pl.multiple_of(start, TILE), sizes[k])

    def place(k):
        last = firsts[k] + sizes[k]
        needed = min(pieces, -(-last // deep))
        while arrived[0] < needed:
            for c in deals[arrived[0]]:
                c.wait_recv()
            arrived[0] += 1
        used = needed * plane * deep
        spots = lax.broadcasted_iota(jnp.int32, (sizes[k], used), 0) + firsts[k]
        pick = jnp.where(spots == target[:, :used], 1.0, 0.0).astype(jnp.bfloat16)
        rows = recv[pl.ds(0, needed)].reshape(used, width)
        kv[region(k, spot), :] = jnp.dot(pick, rows, preferred_element_type=jnp.float32).astype(
            jnp.bfloat16
        )

    def inner(k):
        return pl.ds(firsts[k], sizes[k])

    def up(k):
        return remote(
            kv.at[region(k, spot), :], inbox.at[inner(k), :], up_sem, (k,), {"ctx": me + plane}
        )

    def up_in(k):
        here = inbox.at[inner(k), :]
        return remote(here, here, up_sem, (k,), {"ctx": me - plane})

    def across(k, o):
        here = kv.at[region(k, spot), :]
        return remote(here, here, plane_sem, (k, o), {"ctx": z * plane + (spot ^ o)})

    def across_in(k, o):
        here = kv.at[region(k, spot ^ o), :]
        return remote(here, here, plane_sem, (k, o), {"ctx": z * plane + (spot ^ o)})

    def relay(k, part, peer):
        here = kv.at[region(k, spot ^ peer), pl.ds(part * keyed, keyed)]
        return remote(
            here, here, relay_sem, (k, part), {"ctx": z * plane + (spot ^ (3 - peer))}
        )

    def relay_in(k, part):
        here = kv.at[region(k, spot ^ 3), pl.ds(part * keyed, keyed)]
        return remote(here, here, relay_sem, (k, part), {"ctx": z * plane + (spot ^ 3)})

    def merge(k):
        @pl.when(z > 0)
        def _():
            up_in(k).wait_recv()
            kv[region(k, spot), :] += inbox[inner(k), :]

        @pl.when(z + 1 < lines)
        def _():
            up(k).start()

        for o in direct:
            across(k, o).start()

    def pass_on(k):
        for o in direct:
            across_in(k, o).wait_recv()
        if square:
            for part, peer in ((0, 1), (1, 2)):
                relay(k, part, peer).start()

    def complete(k):
        if square:
            for part in range(2):
                relay_in(k, part).wait_recv()

    ranks = lines * pieces * plane
    lanes = -(-ranks // LANES) * LANES

    def make_names():
        e = lax.broadcasted_iota(jnp.int32, (1, lanes), 1)
        source = e & (plane - 1)
        piece = (e >> shift) & (pieces - 1)
        level = e >> (shift + pieces.bit_length() - 1)
        shard = level * plane + source
        total = jnp.zeros((1, lanes), jnp.int32)
        for d in range(shards):
            number = cnt_all[d, 0:1, :]
            number = jnp.concatenate([number] * (lanes // LANES), axis=1)
            total = jnp.where(shard == d, number, total)
        earlier = jnp.where(
            lax.broadcasted_iota(jnp.int32, (lanes, lanes), 0)
            < lax.broadcasted_iota(jnp.int32, (lanes, lanes), 1),
            1.0,
            0.0,
        ).astype(jnp.bfloat16)
        for line in range(plane):
            mine, skip = dealt_to(line, total, source)
            mine = jnp.clip(mine - deep * piece, 0, deep)
            mine = jnp.where(level <= z, mine, 0)
            start = jnp.dot(
                jnp.broadcast_to(mine.astype(jnp.float32), (8, lanes)).astype(jnp.bfloat16),
                earlier,
                preferred_element_type=jnp.float32,
            )[:1].astype(jnp.int32)
            first_name = shard * slots + plane * deep * piece + skip
            for k in range(steps):
                shape = (sizes[k], lanes)
                within = lax.broadcasted_iota(jnp.int32, shape, 0) + (firsts[k] - start)
                live = (within >= 0) & (within < mine)
                names = jnp.min(
                    jnp.where(live, first_name + plane * within, FAR), axis=1, keepdims=True
                )
                name_s[pl.ds(plane * firsts[k] + line * sizes[k], sizes[k]), :] = jnp.broadcast_to(
                    names, (sizes[k], LANES)
                )

    def attend(k):
        rows = SPAN * sizes[k]

        @pl.loop(0, blocks * (plane // SPAN))
        def _(i):
            b, part = i % blocks, i // blocks
            at = pl.ds(pl.multiple_of(plane * firsts[k] + part * rows, TILE), rows)
            query = me * slots + b * QUERY_BLOCK
            query = query + lax.broadcasted_iota(jnp.int32, (rows, QUERY_BLOCK), 1)
            bias = jnp.where(name_s[at, :] <= query, 0.0, LOW)
            bias = jnp.concatenate([bias] * share, axis=1)
            scores = []
            for g in range(groups):
                key = kv[at, pl.ds(g * HEAD_WIDTH, HEAD_WIDTH)]
                scores.append(
                    lax.dot_general(
                        key, q_s[b, g], (((1,), (1,)), ((), ())), preferred_element_type=jnp.float32
                    )
                    + bias
                )
            for g in range(groups):
                value = kv[at, pl.ds((groups + g) * HEAD_WIDTH, HEAD_WIDTH)]
                old = top_s[b, g]
                top = jnp.maximum(old, jnp.max(scores[g], axis=0, keepdims=True))
                terms = jnp.exp2(scores[g] - top)
                rescale = jnp.exp2(old - top)
                top_s[b, g] = top
                sum_s[b, g] = sum_s[b, g] * rescale + jnp.sum(terms, axis=0, keepdims=True)
                acc_s[b, g] = acc_s[b, g] * rescale + lax.dot_general(
                    value,
                    terms.astype(jnp.bfloat16),
                    (((0,), (0,)), ((), ())),
                    preferred_element_type=jnp.float32,
                )

    place(0)
    for k in range(steps):
        merge(k)
        if k + 1 < steps:
            place(k + 1)
        if k == 0:
            make_names()
        if k >= 1:
            pass_on(k - 1)
        if k >= 2:
            complete(k - 2)
            attend(k - 2)
    pass_on(steps - 1)
    for k in (steps - 2, steps - 1):
        complete(k)
        attend(k)

    loads[4].wait()
    for b in range(blocks):
        at = pl.ds(b * QUERY_BLOCK, QUERY_BLOCK)
        live = b * QUERY_BLOCK + lax.broadcasted_iota(jnp.int32, (LANES, LANES), 0) < count
        gain_s[at, :] = jnp.where(live, as_column(router_s[b : b + 1, :]), 0.0)

    def trade(b):
        at = pl.ds(b * QUERY_BLOCK, QUERY_BLOCK)
        return remote(mine_s.at[at, :], theirs_s.at[at, :], trade_sem, (b,), {"head": other})

    for b in range(blocks):
        at = pl.ds(b * QUERY_BLOCK, QUERY_BLOCK)
        for g in range(groups):
            done = acc_s[b, g] / sum_s[b, g]
            for h in range(share):
                part = done[:, h * QUERY_BLOCK : (h + 1) * QUERY_BLOCK]
                mine_s[at, pl.ds((g * share + h) * HEAD_WIDTH, HEAD_WIDTH)] = part.T.astype(
                    jnp.bfloat16
                )
        trade(b).start()

    tile = min(COLUMN_TILE, half)
    tiles = half // tile
    loads[5].wait()

    @pl.loop(0, tiles)
    def _(n):
        cols = pl.ds(pl.multiple_of(n * tile, tile), tile)
        part_s[:, cols] = jnp.dot(mine_s[...], own_w[:, cols], preferred_element_type=jnp.float32)

    for c in swaps:
        c.wait_recv()
    for b in range(blocks):
        trade(b).wait_recv()
    gain = jnp.concatenate([gain_s[...]] * (tile // LANES), axis=1)
    outs = []
    for n in range(tiles):
        cols = pl.ds(n * tile, tile)
        summed = part_s[:, cols] + jnp.dot(
            theirs_s[...], got_w[:, cols], preferred_element_type=jnp.float32
        )
        summed = summed.astype(jnp.bfloat16).astype(jnp.float32)
        out_s[:, cols] = (gain * summed).astype(jnp.bfloat16)
        outs.append(pltpu.make_async_copy(out_s.at[:, cols], out_ref.at[:, cols], out_sem.at[n]))
        outs[n].start()

    for c in cnt_copies:
        c.wait_send()
    for far in range(lines - 1):
        pl.when((z >= far) & (z + 1 < lines))(lambda: up_counts(far).wait_send())
    for piece in deals:
        for c in piece:
            c.wait_send()
    for k in range(steps):
        pl.when(z + 1 < lines)(lambda: up(k).wait_send())
        for o in direct:
            across(k, o).wait_send()
        if square:
            for part, peer in ((0, 1), (1, 2)):
                relay(k, part, peer).wait_send()
    for c in swaps:
        c.wait_send()
    for b in range(blocks):
        trade(b).wait_send()
    for c in outs:
        c.wait()


def local(q_home, k_home, value_slots_local, out_weight, router, positions, counts):
    shards = lax.axis_size("ctx")
    lines, plane = arrange(shards)
    sizes = plan(shards)
    steps, room = len(sizes), sum(sizes)
    slots, features = q_home.shape
    keyed = k_home.shape[1]
    width = 2 * keyed
    groups = keyed // HEAD_WIDTH
    share = features // HEAD_WIDTH // groups
    stack = share * QUERY_BLOCK
    blocks = slots // QUERY_BLOCK
    half = out_weight.shape[1] // 2
    deep = max(TILE, QUERY_BLOCK // plane)
    pieces = slots // (deep * plane)
    tiles = half // min(COLUMN_TILE, half)
    rows = lambda a: a.reshape(blocks, QUERY_BLOCK)
    vmem, dma = pltpu.VMEM, pltpu.SemaphoreType.DMA
    bf16, f32, i32 = jnp.bfloat16, jnp.float32, jnp.int32
    return pl.pallas_call(
        functools.partial(fused_kernel, shards, sizes),
        out_shape=jax.ShapeDtypeStruct((slots, half), bf16),
        in_specs=[pl.BlockSpec(memory_space=pltpu.SMEM)] + [pl.BlockSpec(memory_space=pl.ANY)] * 6,
        out_specs=pl.BlockSpec(memory_space=pl.ANY),
        scratch_shapes=[
            vmem((slots, width), bf16),
            vmem((slots, features), bf16),
            vmem((blocks, QUERY_BLOCK), i32),
            vmem((blocks, QUERY_BLOCK), f32),
            vmem((slots, HEAD_WIDTH), f32),
            vmem((slots, HEAD_WIDTH), f32),
            vmem((pieces, plane, deep, width), bf16),
            vmem((pieces, plane, deep, width), bf16),
            vmem((room, width), bf16),
            vmem((plane * room, width), bf16),
            vmem((shards, 8, LANES), i32),
            vmem((plane * room, LANES), i32),
            vmem((blocks, groups, stack, HEAD_WIDTH), bf16),
            vmem((blocks, groups, 1, stack), f32),
            vmem((blocks, groups, 1, stack), f32),
            vmem((blocks, groups, HEAD_WIDTH, stack), f32),
            vmem((slots, LANES), f32),
            vmem((features, half), bf16),
            vmem((features, half), bf16),
            vmem((slots, features), bf16),
            vmem((slots, features), bf16),
            vmem((slots, half), f32),
            vmem((slots, half), bf16),
            dma((6,)),
            dma((2, plane)),
            dma((2, lines)),
            dma((2, pieces, plane)),
            dma((2, steps)),
            dma((2, steps, plane)),
            dma((2, steps, 2)),
            dma((2, SWAP_PARTS)),
            dma((2, blocks)),
            dma((tiles,)),
        ],
        compiler_params=pltpu.CompilerParams(collective_id=0, has_side_effects=True),
        name="fused",
    )(
        counts,
        rows(positions),
        rows(router),
        q_home,
        k_home,
        value_slots_local,
        out_weight,
    )


def solution(mesh):
    return jax.shard_map(
        local,
        mesh=mesh,
        in_specs=(
            P("ctx", "head"),
            P("ctx", "head"),
            P("ctx", "head"),
            P("head", None),
            P("ctx"),
            P("ctx"),
            P("ctx"),
        ),
        out_specs=P("ctx", "head"),
        check_vma=False,
    )
```

time: 82.3 us -> 59.8 us (0.73)
  the two profiles are of different devices: /device:TPU:23 before, /device:TPU:24 now
where the time goes in v1:
time: 59.8 us; the launch traced here: 59.6 us
  Pallas kernels  55.8 us (93%)
  local copies, waits for them, and re-layouts  3.16 us (5%)
  between operations  0.66 us (1%)
    pallas_call x1, Pallas kernels, local(): pl.pallas_call(functools.partial(fused_kernel, shards, sizes), out_shape=...  55.8 us
    unnamed x1, local copies, waits for them, and re-layouts  3.16 us

profile of v1, /device:TPU:24, one launch (start us, length us, event | category | flops | bytes accessed | tf_op | source)
XLA Modules:
  0.0 59.6 jit_solution(11686451209175891919)
XLA Ops:
  0.7 55.8 %fused.1 = bf16[512,2048]{1,0:T(8,128)(2,1)} custom-call(s32[1]{0:T(128)S(6)} %copy.9.count_ref, s32[4,128]{1,0:T(4,128)} %bitcast.2, f32[4,128]{1,0:T(4,128)} %bitcast.3, bf16[512,1024]{1,0:T(8,128)(2,1)} %q_ref.1, bf16[512,256]{1,0:T(8,128)(2,1)} %k_ref.1, bf16[512,256]{1,0:T(8,128)(2,1)} %v_ref.1, bf16[1024,4096]{1,0:T(8,128)(2,1)} %weight_ref.1), custom_call_target="tpu_custom_call" | custom-call | tf_op jit(solution)/shard_map/fused/pallas_call | solution.py:568
  56.5 3.2 %copy.10 = bf16[512,2048]{1,0:T(8,128)(2,1)} copy(bf16[512,2048]{1,0:T(8,128)(2,1)} %fused.1) | data formatting | bytes 4194304

commit v2 on v1

--- a/solution.py
+++ b/solution.py
@@ -16,6 +16,10 @@
 LANES = 128
 COLUMN_TILE = 512
 SPAN = 4
+STEP = 48
+PASS_LAG = 3
+DONE_LAG = 3
+SPARE = 10 << 20
 FAR = 1 << 28
 LOW = -1e30
 QUARTER = 1 << 30
@@ -63,10 +67,23 @@
     lines, plane = arrange(shards)
     most = PICKED_PER_SHARD * lines + lines * (plane - 1) // 2
     room = -(-most // TILE) * TILE
-    step = 96 if plane == 4 else 128
-    sizes = [room % step] if room % step else []
-    sizes += [step] * (room // step)
+    step = STEP if plane == SPAN else 2 * STEP
+    sizes = []
+    while sum(sizes) < room:
+        grown = TILE << len(sizes) if plane == SPAN else step
+        sizes.append(min(grown, step, room - sum(sizes)))
     return tuple(sizes)
+
+
+def gather_up(sizes):
+    most = 2 * STEP if len(sizes) > 2 and max(sizes) <= STEP else max(sizes)
+    groups, held = [], []
+    for k, size in enumerate(sizes):
+        if held and (sum(sizes[i] for i in held) + size > most or k == len(sizes) - 1):
+            groups.append(held)
+            held = []
+        held.append(k)
+    return groups + [held]
 
 
 def fused_kernel(
@@ -102,7 +119,6 @@
     mine_s,
     theirs_s,
     part_s,
-    out_s,
     load_sem,
     cnt_sem,
     up_cnt_sem,
@@ -112,8 +128,7 @@
     relay_sem,
     swap_sem,
     trade_sem,
-    out_sem,
-):
+    ):
     lines, plane = arrange(shards)
     shift = plane.bit_length() - 1
     me = lax.axis_index("ctx")
@@ -426,13 +441,14 @@
                     names, (sizes[k], LANES)
                 )
 
-    def attend(k):
-        rows = SPAN * sizes[k]
-
-        @pl.loop(0, blocks * (plane // SPAN))
+    def attend(members, final=False):
+        rows = SPAN * sum(sizes[k] for k in members)
+        parts = plane // SPAN
+
+        @pl.loop(0, blocks * parts)
         def _(i):
             b, part = i % blocks, i // blocks
-            at = pl.ds(pl.multiple_of(plane * firsts[k] + part * rows, TILE), rows)
+            at = pl.ds(pl.multiple_of(plane * firsts[members[0]] + part * rows, TILE), rows)
             query = me * slots + b * QUERY_BLOCK
             query = query + lax.broadcasted_iota(jnp.int32, (rows, QUERY_BLOCK), 1)
             bias = jnp.where(name_s[at, :] <= query, 0.0, LOW)
@@ -460,23 +476,24 @@
                     (((0,), (0,)), ((), ())),
                     preferred_element_type=jnp.float32,
                 )
-
-    place(0)
-    for k in range(steps):
-        merge(k)
-        if k + 1 < steps:
-            place(k + 1)
-        if k == 0:
-            make_names()
-        if k >= 1:
-            pass_on(k - 1)
-        if k >= 2:
-            complete(k - 2)
-            attend(k - 2)
-    pass_on(steps - 1)
-    for k in (steps - 2, steps - 1):
-        complete(k)
-        attend(k)
+            if final:
+                pl.when(part == parts - 1)(functools.partial(finish, b))
+
+    def block_rows(b):
+        return pl.ds(pl.multiple_of(b * QUERY_BLOCK, QUERY_BLOCK), QUERY_BLOCK)
+
+    def trade(b):
+        at = block_rows(b)
+        return remote(mine_s.at[at, :], theirs_s.at[at, :], trade_sem, (b,), {"head": other})
+
+    def finish(b):
+        for g in range(groups):
+            done = acc_s[b, g] / sum_s[b, g]
+            for h in range(share):
+                part = done[:, h * QUERY_BLOCK : (h + 1) * QUERY_BLOCK]
+                cols = pl.ds((g * share + h) * HEAD_WIDTH, HEAD_WIDTH)
+                mine_s[block_rows(b), cols] = part.T.astype(jnp.bfloat16)
+        trade(b).start()
 
     loads[4].wait()
     for b in range(blocks):
@@ -484,20 +501,32 @@
         live = b * QUERY_BLOCK + lax.broadcasted_iota(jnp.int32, (LANES, LANES), 0) < count
         gain_s[at, :] = jnp.where(live, as_column(router_s[b : b + 1, :]), 0.0)
 
-    def trade(b):
-        at = pl.ds(b * QUERY_BLOCK, QUERY_BLOCK)
-        return remote(mine_s.at[at, :], theirs_s.at[at, :], trade_sem, (b,), {"head": other})
-
-    for b in range(blocks):
-        at = pl.ds(b * QUERY_BLOCK, QUERY_BLOCK)
-        for g in range(groups):
-            done = acc_s[b, g] / sum_s[b, g]
-            for h in range(share):
-                part = done[:, h * QUERY_BLOCK : (h + 1) * QUERY_BLOCK]
-                mine_s[at, pl.ds((g * share + h) * HEAD_WIDTH, HEAD_WIDTH)] = part.T.astype(
-                    jnp.bfloat16
-                )
-        trade(b).start()
+    place(0)
+    pl.when(z > 0)(make_names)
+    waiting = gather_up(sizes)
+    completed = [0]
+
+    def attend_ready(upto):
+        while waiting and waiting[0][-1] <= upto:
+            members = waiting.pop(0)
+            while completed[0] <= members[-1]:
+                complete(completed[0])
+                completed[0] += 1
+            attend(members, not waiting)
+
+    for k in range(steps):
+        merge(k)
+        if k + 1 < steps:
+            place(k + 1)
+        if k == 1:
+            pl.when(z == 0)(make_names)
+        if k >= PASS_LAG:
+            pass_on(k - PASS_LAG)
+        attend_ready(k - PASS_LAG - DONE_LAG)
+    for k in range(max(0, steps - PASS_LAG), steps):
+        pass_on(k)
+        attend_ready(k - DONE_LAG)
+    attend_ready(steps - 1)
 
     tile = min(COLUMN_TILE, half)
     tiles = half // tile
@@ -513,16 +542,13 @@
     for b in range(blocks):
         trade(b).wait_recv()
     gain = jnp.concatenate([gain_s[...]] * (tile // LANES), axis=1)
-    outs = []
     for n in range(tiles):
         cols = pl.ds(n * tile, tile)
         summed = part_s[:, cols] + jnp.dot(
             theirs_s[...], got_w[:, cols], preferred_element_type=jnp.float32
         )
         summed = summed.astype(jnp.bfloat16).astype(jnp.float32)
-        out_s[:, cols] = (gain * summed).astype(jnp.bfloat16)
-        outs.append(pltpu.make_async_copy(out_s.at[:, cols], out_ref.at[:, cols], out_sem.at[n]))
-        outs[n].start()
+        out_ref[:, cols] = (gain * summed).astype(jnp.bfloat16)
 
     for c in cnt_copies:
         c.wait_send()
@@ -542,8 +568,6 @@
         c.wait_send()
     for b in range(blocks):
         trade(b).wait_send()
-    for c in outs:
-        c.wait()
 
 
 def local(q_home, k_home, value_slots_local, out_weight, router, positions, counts):
@@ -561,60 +585,63 @@
     half = out_weight.shape[1] // 2
     deep = max(TILE, QUERY_BLOCK // plane)
     pieces = slots // (deep * plane)
-    tiles = half // min(COLUMN_TILE, half)
     rows = lambda a: a.reshape(blocks, QUERY_BLOCK)
     vmem, dma = pltpu.VMEM, pltpu.SemaphoreType.DMA
     bf16, f32, i32 = jnp.bfloat16, jnp.float32, jnp.int32
+    scratch = [
+        vmem((slots, width), bf16),
+        vmem((slots, features), bf16),
+        vmem((blocks, QUERY_BLOCK), i32),
+        vmem((blocks, QUERY_BLOCK), f32),
+        vmem((slots, HEAD_WIDTH), f32),
+        vmem((slots, HEAD_WIDTH), f32),
+        vmem((pieces, plane, deep, width), bf16),
+        vmem((pieces, plane, deep, width), bf16),
+        vmem((room, width), bf16),
+        vmem((plane * room, width), bf16),
+        vmem((shards, 8, LANES), i32),
+        vmem((plane * room, LANES), i32),
+        vmem((blocks, groups, stack, HEAD_WIDTH), bf16),
+        vmem((blocks, groups, 1, stack), f32),
+        vmem((blocks, groups, 1, stack), f32),
+        vmem((blocks, groups, HEAD_WIDTH, stack), f32),
+        vmem((slots, LANES), f32),
+        vmem((features, half), bf16),
+        vmem((features, half), bf16),
+        vmem((slots, features), bf16),
+        vmem((slots, features), bf16),
+        vmem((slots, half), f32),
+        dma((6,)),
+        dma((2, plane)),
+        dma((2, lines)),
+        dma((2, pieces, plane)),
+        dma((2, steps)),
+        dma((2, steps, plane)),
+        dma((2, steps, 2)),
+        dma((2, SWAP_PARTS)),
+        dma((2, blocks)),
+    ]
+    buffers = [m for m in scratch if m.memory_space == pltpu.VMEM]
+    taken = sum(math.prod(m.shape) * jnp.dtype(m.dtype).itemsize for m in buffers)
+    placed = lambda a: pltpu.with_memory_space_constraint(a, pltpu.HBM)
     return pl.pallas_call(
         functools.partial(fused_kernel, shards, sizes),
         out_shape=jax.ShapeDtypeStruct((slots, half), bf16),
         in_specs=[pl.BlockSpec(memory_space=pltpu.SMEM)] + [pl.BlockSpec(memory_space=pl.ANY)] * 6,
-        out_specs=pl.BlockSpec(memory_space=pl.ANY),
-        scratch_shapes=[
-            vmem((slots, width), bf16),
-            vmem((slots, features), bf16),
-            vmem((blocks, QUERY_BLOCK), i32),
-            vmem((blocks, QUERY_BLOCK), f32),
-            vmem((slots, HEAD_WIDTH), f32),
-            vmem((slots, HEAD_WIDTH), f32),
-            vmem((pieces, plane, deep, width), bf16),
-            vmem((pieces, plane, deep, width), bf16),
-            vmem((room, width), bf16),
-            vmem((plane * room, width), bf16),
-            vmem((shards, 8, LANES), i32),
-            vmem((plane * room, LANES), i32),
-            vmem((blocks, groups, stack, HEAD_WIDTH), bf16),
-            vmem((blocks, groups, 1, stack), f32),
-            vmem((blocks, groups, 1, stack), f32),
-            vmem((blocks, groups, HEAD_WIDTH, stack), f32),
-            vmem((slots, LANES), f32),
-            vmem((features, half), bf16),
-            vmem((features, half), bf16),
-            vmem((slots, features), bf16),
-            vmem((slots, features), bf16),
-            vmem((slots, half), f32),
-            vmem((slots, half), bf16),
-            dma((6,)),
-            dma((2, plane)),
-            dma((2, lines)),
-            dma((2, pieces, plane)),
-            dma((2, steps)),
-            dma((2, steps, plane)),
-            dma((2, steps, 2)),
-            dma((2, SWAP_PARTS)),
-            dma((2, blocks)),
-            dma((tiles,)),
-        ],
-        compiler_params=pltpu.CompilerParams(collective_id=0, has_side_effects=True),
+        out_specs=pl.BlockSpec(memory_space=pltpu.VMEM),
+        scratch_shapes=scratch,
+        compiler_params=pltpu.CompilerParams(
+            collective_id=0, has_side_effects=True, vmem_limit_bytes=taken + SPARE
+        ),
         name="fused",
     )(
         counts,
-        rows(positions),
-        rows(router),
-        q_home,
-        k_home,
-        value_slots_local,
-        out_weight,
+        placed(rows(positions)),
+        placed(rows(router)),
+        placed(q_home),
+        placed(k_home),
+        placed(value_slots_local),
+        placed(out_weight),
     )
 
 

time: 59.8 us -> 56.1 us (0.938)
  local copies, waits for them, and re-layouts: 3.16 us -> 1.32 us
  Pallas kernels: 55.8 us -> 54 us
    unnamed x1, local copies, waits for them, and re-layouts: 3.16 us -> 1.32 us
    pallas_call x1, Pallas kernels: 55.8 us -> 54 us  [local(): pl.pallas_call(functools.partial(fused_kernel, shards, sizes), out_shape=...]
where the time goes in v2:
time: 56.1 us; the launch traced here: 56 us
  Pallas kernels  54 us (96%)
  local copies, waits for them, and re-layouts  1.32 us (2%)
  between operations  0.66 us (1%)
    pallas_call x1, Pallas kernels, local(): pl.pallas_call(functools.partial(fused_kernel, shards, sizes), out_shape=...  54 us
    unnamed x1, local copies, waits for them, and re-layouts  1.32 us

profile of v2, /device:TPU:24, one launch (start us, length us, event | category | flops | bytes accessed | tf_op | source)
XLA Modules:
  0.0 56.0 jit_solution(3681949227476869708)
XLA Ops:
  0.7 54.0 %fused.1 = bf16[512,2048]{1,0:T(8,128)(2,1)S(1)} custom-call(s32[1]{0:T(128)S(6)} %copy.9.count_ref, s32[4,128]{1,0:T(4,128)} %bitcast.2, f32[4,128]{1,0:T(4,128)} %bitcast.3, bf16[512,1024]{1,0:T(8,128)(2,1)} %q_ref.1, bf16[512,256]{1,0:T(8,128)(2,1)} %k_ref.1, bf16[512,256]{1,0:T(8,128)(2,1)} %v_ref.1, bf16[1024,4096]{1,0:T(8,128)(2,1)} %weight_ref.1), custom_call_target="tpu_custom_call" | custom-call | tf_op jit(solution)/shard_map/fused/pallas_call | solution.py:627
  54.6 1.3 %copy.10 = bf16[512,2048]{1,0:T(8,128)(2,1)} copy(bf16[512,2048]{1,0:T(8,128)(2,1)S(1)} %fused.1) | data formatting | bytes 4194304

commit v3 on v2

--- a/solution.py
+++ b/solution.py
@@ -17,8 +17,15 @@
 COLUMN_TILE = 512
 SPAN = 4
 STEP = 48
+UNIT_MOST = 768
+UNIT_LEAST = 288
+ROW_TIME = 0.022
+CHAIN_TIME = 0.024
+HOP_TIME = 1.7
+MERGE_COST = 0.3
+UNIT_COST = 0.2
+KEY_COST = 0.0016
 PASS_LAG = 3
-DONE_LAG = 3
 SPARE = 10 << 20
 FAR = 1 << 28
 LOW = -1e30
@@ -75,15 +82,69 @@
     return tuple(sizes)
 
 
-def gather_up(sizes):
-    most = 2 * STEP if len(sizes) > 2 and max(sizes) <= STEP else max(sizes)
-    groups, held = [], []
-    for k, size in enumerate(sizes):
-        if held and (sum(sizes[i] for i in held) + size > most or k == len(sizes) - 1):
-            groups.append(held)
-            held = []
-        held.append(k)
-    return groups + [held]
+def timetable(sizes, blocks):
+    steps = len(sizes)
+    firsts = [sum(sizes[:i]) for i in range(steps)]
+    merge_at = [CHAIN_TIME * (firsts[k] + sizes[k]) for k in range(steps)]
+    pass_at, done_at = {}, {}
+    events, now, link = [], 0.0, 0.0
+    merged = passed = done = 0
+    pending = [[] for _ in range(blocks)]
+
+    def owed(b):
+        return sum(size for _, _, size in pending[b])
+
+    def attend(b, final=False):
+        taken = []
+        while pending[b] and (final or sum(t[2] for t in taken) + pending[b][0][2] <= UNIT_MOST):
+            taken.append(pending[b].pop(0))
+        spans = []
+        for o, start, size in sorted(taken):
+            if spans and spans[-1][0] == o and spans[-1][1] + spans[-1][2] == start:
+                spans[-1][2] += size
+            else:
+                spans.append([o, start, size])
+        events.append(("attend", b, spans, final))
+        return UNIT_COST + KEY_COST * sum(t[2] for t in taken)
+
+    def found(o, k):
+        for rows in pending:
+            rows.append((o, firsts[k], sizes[k]))
+
+    while done < steps:
+        if merged < steps and merge_at[merged] <= now:
+            events.append(("merge", merged))
+            now += MERGE_COST
+            link = max(link, now) + ROW_TIME * sizes[merged]
+            pass_at[merged] = link + HOP_TIME
+            found(0, merged)
+            merged += 1
+            continue
+        if passed in pass_at and pass_at[passed] <= now:
+            events.append(("pass", passed))
+            link = max(link, now) + ROW_TIME * sizes[passed] / 2
+            done_at[passed] = link + HOP_TIME
+            found(1, passed)
+            found(2, passed)
+            passed += 1
+            continue
+        if done in done_at and done_at[done] <= now:
+            events.append(("done", done))
+            found(3, done)
+            done += 1
+            continue
+        b = max(range(blocks), key=owed)
+        coming = [done_at[done]] if done in done_at else []
+        coming += [pass_at[passed]] if passed in pass_at else []
+        coming += [merge_at[merged]] if merged < steps else []
+        gap = min(coming) - now
+        if owed(b) >= UNIT_LEAST or (owed(b) and gap > UNIT_COST + KEY_COST * owed(b)):
+            now += attend(b)
+        else:
+            now += gap
+    for b in range(blocks):
+        attend(b, True)
+    return events
 
 
 def fused_kernel(
@@ -326,9 +387,8 @@
 
     arrived = [0]
 
-    def region(k, line):
-        start = plane * firsts[k] + line * sizes[k]
-        return pl.ds(pl.multiple_of(start, TILE), sizes[k])
+    def inner(k):
+        return pl.ds(firsts[k], sizes[k])
 
     def place(k):
         last = firsts[k] + sizes[k]
@@ -341,16 +401,13 @@
         spots = lax.broadcasted_iota(jnp.int32, (sizes[k], used), 0) + firsts[k]
         pick = jnp.where(spots == target[:, :used], 1.0, 0.0).astype(jnp.bfloat16)
         rows = recv[pl.ds(0, needed)].reshape(used, width)
-        kv[region(k, spot), :] = jnp.dot(pick, rows, preferred_element_type=jnp.float32).astype(
+        kv[spot, inner(k), :] = jnp.dot(pick, rows, preferred_element_type=jnp.float32).astype(
             jnp.bfloat16
         )
 
-    def inner(k):
-        return pl.ds(firsts[k], sizes[k])
-
     def up(k):
         return remote(
-            kv.at[region(k, spot), :], inbox.at[inner(k), :], up_sem, (k,), {"ctx": me + plane}
+            kv.at[spot, inner(k), :], inbox.at[inner(k), :], up_sem, (k,), {"ctx": me + plane}
         )
 
     def up_in(k):
@@ -358,28 +415,28 @@
         return remote(here, here, up_sem, (k,), {"ctx": me - plane})
 
     def across(k, o):
-        here = kv.at[region(k, spot), :]
+        here = kv.at[spot, inner(k), :]
         return remote(here, here, plane_sem, (k, o), {"ctx": z * plane + (spot ^ o)})
 
     def across_in(k, o):
-        here = kv.at[region(k, spot ^ o), :]
+        here = kv.at[spot ^ o, inner(k), :]
         return remote(here, here, plane_sem, (k, o), {"ctx": z * plane + (spot ^ o)})
 
     def relay(k, part, peer):
-        here = kv.at[region(k, spot ^ peer), pl.ds(part * keyed, keyed)]
+        here = kv.at[spot ^ peer, inner(k), pl.ds(part * keyed, keyed)]
         return remote(
             here, here, relay_sem, (k, part), {"ctx": z * plane + (spot ^ (3 - peer))}
         )
 
     def relay_in(k, part):
-        here = kv.at[region(k, spot ^ 3), pl.ds(part * keyed, keyed)]
+        here = kv.at[spot ^ 3, inner(k), pl.ds(part * keyed, keyed)]
         return remote(here, here, relay_sem, (k, part), {"ctx": z * plane + (spot ^ 3)})
 
     def merge(k):
         @pl.when(z > 0)
         def _():
             up_in(k).wait_recv()
-            kv[region(k, spot), :] += inbox[inner(k), :]
+            kv[spot, inner(k), :] += inbox[inner(k), :]
 
         @pl.when(z + 1 < lines)
         def _():
@@ -420,7 +477,9 @@
             1.0,
             0.0,
         ).astype(jnp.bfloat16)
-        for line in range(plane):
+
+        @pl.loop(0, plane)
+        def _(line):
             mine, skip = dealt_to(line, total, source)
             mine = jnp.clip(mine - deep * piece, 0, deep)
             mine = jnp.where(level <= z, mine, 0)
@@ -430,54 +489,46 @@
                 preferred_element_type=jnp.float32,
             )[:1].astype(jnp.int32)
             first_name = shard * slots + plane * deep * piece + skip
-            for k in range(steps):
-                shape = (sizes[k], lanes)
-                within = lax.broadcasted_iota(jnp.int32, shape, 0) + (firsts[k] - start)
-                live = (within >= 0) & (within < mine)
-                names = jnp.min(
-                    jnp.where(live, first_name + plane * within, FAR), axis=1, keepdims=True
+            within = lax.broadcasted_iota(jnp.int32, (room, lanes), 0) - start
+            live = (within >= 0) & (within < mine)
+            names = jnp.min(
+                jnp.where(live, first_name + plane * within, FAR), axis=1, keepdims=True
+            )
+            name_s[line] = jnp.broadcast_to(names, (room, LANES))
+
+    def attend(b, pieces_of):
+        spots = [(line, pl.ds(start, size)) for line, start, size in pieces_of]
+        rows = sum(size for _, _, size in pieces_of)
+
+        def read(ref, cols):
+            return jnp.concatenate([ref[line, at, cols] for line, at in spots], axis=0)
+
+        query = me * slots + b * QUERY_BLOCK
+        query = query + lax.broadcasted_iota(jnp.int32, (rows, QUERY_BLOCK), 1)
+        bias = jnp.where(read(name_s, pl.ds(0, LANES)) <= query, 0.0, LOW)
+        bias = jnp.concatenate([bias] * share, axis=1)
+        scores = []
+        for g in range(groups):
+            key = read(kv, pl.ds(g * HEAD_WIDTH, HEAD_WIDTH))
+            scores.append(
+                lax.dot_general(
+                    key, q_s[b, g], (((1,), (1,)), ((), ())), preferred_element_type=jnp.float32
                 )
-                name_s[pl.ds(plane * firsts[k] + line * sizes[k], sizes[k]), :] = jnp.broadcast_to(
-                    names, (sizes[k], LANES)
-                )
-
-    def attend(members, final=False):
-        rows = SPAN * sum(sizes[k] for k in members)
-        parts = plane // SPAN
-
-        @pl.loop(0, blocks * parts)
-        def _(i):
-            b, part = i % blocks, i // blocks
-            at = pl.ds(pl.multiple_of(plane * firsts[members[0]] + part * rows, TILE), rows)
-            query = me * slots + b * QUERY_BLOCK
-            query = query + lax.broadcasted_iota(jnp.int32, (rows, QUERY_BLOCK), 1)
-            bias = jnp.where(name_s[at, :] <= query, 0.0, LOW)
-            bias = jnp.concatenate([bias] * share, axis=1)
-            scores = []
-            for g in range(groups):
-                key = kv[at, pl.ds(g * HEAD_WIDTH, HEAD_WIDTH)]
-                scores.append(
-                    lax.dot_general(
-                        key, q_s[b, g], (((1,), (1,)), ((), ())), preferred_element_type=jnp.float32
-                    )
-                    + bias
-                )
-            for g in range(groups):
-                value = kv[at, pl.ds((groups + g) * HEAD_WIDTH, HEAD_WIDTH)]
-                old = top_s[b, g]
-                top = jnp.maximum(old, jnp.max(scores[g], axis=0, keepdims=True))
-                terms = jnp.exp2(scores[g] - top)
-                rescale = jnp.exp2(old - top)
-                top_s[b, g] = top
-                sum_s[b, g] = sum_s[b, g] * rescale + jnp.sum(terms, axis=0, keepdims=True)
-                acc_s[b, g] = acc_s[b, g] * rescale + lax.dot_general(
-                    value,
-                    terms.astype(jnp.bfloat16),
-                    (((0,), (0,)), ((), ())),
-                    preferred_element_type=jnp.float32,
-                )
-            if final:
-                pl.when(part == parts - 1)(functools.partial(finish, b))
+                + bias
+            )
+        for g in range(groups):
+            value = read(kv, pl.ds((groups + g) * HEAD_WIDTH, HEAD_WIDTH))
+            value = jnp.concatenate([value, jnp.ones((rows, 8), jnp.bfloat16)], axis=1)
+            old = top_s[b, g]
+            top = jnp.maximum(old, jnp.max(scores[g], axis=0, keepdims=True))
+            terms = jnp.exp2(scores[g] - top).astype(jnp.bfloat16)
+            rescale = jnp.exp2(old - top)
+            added = lax.dot_general(
+                value, terms, (((0,), (0,)), ((), ())), preferred_element_type=jnp.float32
+            )
+            top_s[b, g] = top
+            sum_s[b, g] = sum_s[b, g] * rescale + added[HEAD_WIDTH : HEAD_WIDTH + 1]
+            acc_s[b, g] = acc_s[b, g] * rescale + added[:HEAD_WIDTH]
 
     def block_rows(b):
         return pl.ds(pl.multiple_of(b * QUERY_BLOCK, QUERY_BLOCK), QUERY_BLOCK)
@@ -503,30 +554,47 @@
 
     place(0)
     pl.when(z > 0)(make_names)
-    waiting = gather_up(sizes)
-    completed = [0]
-
-    def attend_ready(upto):
-        while waiting and waiting[0][-1] <= upto:
-            members = waiting.pop(0)
-            while completed[0] <= members[-1]:
-                complete(completed[0])
-                completed[0] += 1
-            attend(members, not waiting)
-
-    for k in range(steps):
+
+    def step(k):
         merge(k)
         if k + 1 < steps:
             place(k + 1)
-        if k == 1:
-            pl.when(z == 0)(make_names)
-        if k >= PASS_LAG:
-            pass_on(k - PASS_LAG)
-        attend_ready(k - PASS_LAG - DONE_LAG)
-    for k in range(max(0, steps - PASS_LAG), steps):
-        pass_on(k)
-        attend_ready(k - DONE_LAG)
-    attend_ready(steps - 1)
+
+    if square:
+        named = False
+        for kind, at, *rest in timetable(sizes, blocks):
+            if kind == "merge":
+                step(at)
+            elif kind == "pass":
+                pass_on(at)
+            elif kind == "done":
+                complete(at)
+            else:
+                if not named:
+                    pl.when(z == 0)(make_names)
+                    named = True
+                spans, final = rest
+                attend(at, [(spot ^ o, start, size) for o, start, size in spans])
+                if final:
+                    finish(at)
+    else:
+        parts = plane // SPAN
+        for k in range(steps + PASS_LAG):
+            if k < steps:
+                step(k)
+            at = k - PASS_LAG
+            if at < 0:
+                continue
+            if at == 0:
+                pl.when(z == 0)(make_names)
+            pass_on(at)
+
+            @pl.loop(0, blocks * parts)
+            def _(i):
+                b, part = i % blocks, i // blocks
+                attend(b, [(part * SPAN + j, firsts[at], sizes[at]) for j in range(SPAN)])
+                if at == steps - 1:
+                    pl.when(part == parts - 1)(functools.partial(finish, b))
 
     tile = min(COLUMN_TILE, half)
     tiles = half // tile
@@ -598,9 +666,9 @@
         vmem((pieces, plane, deep, width), bf16),
         vmem((pieces, plane, deep, width), bf16),
         vmem((room, width), bf16),
-        vmem((plane * room, width), bf16),
+        vmem((plane, room, width), bf16),
         vmem((shards, 8, LANES), i32),
-        vmem((plane * room, LANES), i32),
+        vmem((plane, room, LANES), i32),
         vmem((blocks, groups, stack, HEAD_WIDTH), bf16),
         vmem((blocks, groups, 1, stack), f32),
         vmem((blocks, groups, 1, stack), f32),

time: 56.1 us -> 51.7 us (0.922)
  Pallas kernels: 54 us -> 49.5 us
    pallas_call x1, Pallas kernels: 54 us -> 49.5 us  [local(): pl.pallas_call(functools.partial(fused_kernel, shards, sizes), out_shape=...]
where the time goes in v3:
time: 51.7 us; the launch traced here: 51.5 us
  Pallas kernels  49.5 us (96%)
  local copies, waits for them, and re-layouts  1.32 us (3%)
  between operations  0.66 us (1%)
    pallas_call x1, Pallas kernels, local(): pl.pallas_call(functools.partial(fused_kernel, shards, sizes), out_shape=...  49.5 us
    unnamed x1, local copies, waits for them, and re-layouts  1.32 us

profile of v3, /device:TPU:24, one launch (start us, length us, event | category | flops | bytes accessed | tf_op | source)
XLA Modules:
  0.0 51.5 jit_solution(10274019712584947783)
XLA Ops:
  0.7 49.5 %fused.1 = bf16[512,2048]{1,0:T(8,128)(2,1)S(1)} custom-call(s32[1]{0:T(128)S(6)} %copy.9.count_ref, s32[4,128]{1,0:T(4,128)} %bitcast.2, f32[4,128]{1,0:T(4,128)} %bitcast.3, bf16[512,1024]{1,0:T(8,128)(2,1)} %q_ref.1, bf16[512,256]{1,0:T(8,128)(2,1)} %k_ref.1, bf16[512,256]{1,0:T(8,128)(2,1)} %v_ref.1, bf16[1024,4096]{1,0:T(8,128)(2,1)} %weight_ref.1), custom_call_target="tpu_custom_call" | custom-call | tf_op jit(solution)/shard_map/fused/pallas_call | solution.py:695
  50.2 1.3 %copy.10 = bf16[512,2048]{1,0:T(8,128)(2,1)} copy(bf16[512,2048]{1,0:T(8,128)(2,1)S(1)} %fused.1) | data formatting | bytes 4194304

commit v4 on v3

--- a/solution.py
+++ b/solution.py
@@ -19,9 +19,10 @@
 STEP = 48
 UNIT_MOST = 768
 UNIT_LEAST = 288
+UNIT_SPARE = 96
 ROW_TIME = 0.022
 CHAIN_TIME = 0.024
-HOP_TIME = 1.7
+HOP_TIME = 1.8
 MERGE_COST = 0.3
 UNIT_COST = 0.2
 KEY_COST = 0.0016
@@ -138,7 +139,8 @@
         coming += [pass_at[passed]] if passed in pass_at else []
         coming += [merge_at[merged]] if merged < steps else []
         gap = min(coming) - now
-        if owed(b) >= UNIT_LEAST or (owed(b) and gap > UNIT_COST + KEY_COST * owed(b)):
+        spare = gap > UNIT_COST + KEY_COST * owed(b)
+        if owed(b) >= UNIT_LEAST or (owed(b) >= UNIT_SPARE and spare):
             now += attend(b)
         else:
             now += gap
@@ -248,21 +250,45 @@
         rate = jnp.where((lane & (HEAD_WIDTH // 2 - 1)) == i, value, rate)
     lead = jnp.where(lane < HEAD_WIDTH // 2, QUARTER, -QUARTER)
     loads[0].wait()
-    for b in range(blocks):
-        at = pl.ds(b * QUERY_BLOCK, QUERY_BLOCK)
-        column = as_column(pos_s[b : b + 1, :].astype(jnp.float32)).astype(jnp.int32)
-        phase = column * rate
-        cos_s[at, :] = cosine_of(phase)
-        sin_s[at, :] = cosine_of(phase + lead)
-
-    loads[1].wait()
-    loads[2].wait()
     block = plane * deep
     row = lax.broadcasted_iota(jnp.int32, (block, block), 0)
     column = lax.broadcasted_iota(jnp.int32, (block, block), 1)
     chosen = column == plane * (row % deep) + row // deep
     deal_map = jnp.where(chosen, 1.0, 0.0).astype(jnp.bfloat16)
+
+    def mate(o):
+        return {"ctx": z * plane + ((spot + o) & (plane - 1))}
+
+    def remote(src, dst, sems, index, target):
+        return pltpu.make_async_remote_copy(
+            src_ref=src,
+            dst_ref=dst,
+            send_sem=sems.at[(0,) + index],
+            recv_sem=sems.at[(1,) + index],
+            device_id=target,
+        )
+
+    cnt_copies = [
+        remote(cnt_all.at[me], cnt_all.at[me], cnt_sem, (o,), mate(o)) for o in range(1, plane)
+    ]
+    deals = [
+        [
+            remote(send.at[t, o], recv.at[t, spot], deal_sem, (t, o), mate(o))
+            for o in range(1, plane)
+        ]
+        for t in range(pieces)
+    ]
+    greeted = plane + (z > 0).astype(jnp.int32) + (z + 1 < lines).astype(jnp.int32)
     for t in range(pieces):
+        for b in range(t * block // QUERY_BLOCK, (t + 1) * block // QUERY_BLOCK):
+            at = pl.ds(b * QUERY_BLOCK, QUERY_BLOCK)
+            column = as_column(pos_s[b : b + 1, :].astype(jnp.float32)).astype(jnp.int32)
+            phase = column * rate
+            cos_s[at, :] = cosine_of(phase)
+            sin_s[at, :] = cosine_of(phase + lead)
+        if t == 0:
+            loads[1].wait()
+            loads[2].wait()
         at = pl.ds(t * block, block)
         parts = []
         for c in range(keyed // HEAD_WIDTH):
@@ -272,36 +298,11 @@
         rows = jnp.concatenate(parts, axis=1)
         dealt = jnp.dot(deal_map, rows, preferred_element_type=jnp.float32)
         send[t] = dealt.astype(jnp.bfloat16).reshape(plane, deep, width)
-
-    greeted = plane + (z > 0).astype(jnp.int32) + (z + 1 < lines).astype(jnp.int32)
-    pl.semaphore_wait(barrier, greeted)
-
-    def mate(o):
-        return {"ctx": z * plane + ((spot + o) & (plane - 1))}
-
-    def remote(src, dst, sems, index, target):
-        return pltpu.make_async_remote_copy(
-            src_ref=src,
-            dst_ref=dst,
-            send_sem=sems.at[(0,) + index],
-            recv_sem=sems.at[(1,) + index],
-            device_id=target,
-        )
-
-    cnt_copies = [
-        remote(cnt_all.at[me], cnt_all.at[me], cnt_sem, (o,), mate(o)) for o in range(1, plane)
-    ]
-    for c in cnt_copies:
-        c.start()
-    deals = [
-        [
-            remote(send.at[t, o], recv.at[t, spot], deal_sem, (t, o), mate(o))
-            for o in range(1, plane)
-        ]
-        for t in range(pieces)
-    ]
-    for piece in deals:
-        for c in piece:
+        if t == 0:
+            pl.semaphore_wait(barrier, greeted)
+            for c in cnt_copies:
+                c.start()
+        for c in deals[t]:
             c.start()
     for t in range(pieces):
         recv[t, spot] = send[t, 0]
@@ -552,16 +553,28 @@
         live = b * QUERY_BLOCK + lax.broadcasted_iota(jnp.int32, (LANES, LANES), 0) < count
         gain_s[at, :] = jnp.where(live, as_column(router_s[b : b + 1, :]), 0.0)
 
-    place(0)
-    pl.when(z > 0)(make_names)
+    @pl.when(z == 0)
+    def _():
+        for k in range(steps):
+            place(k)
+            merge(k)
+        make_names()
+
+    arrived[0] = 0
+
+    @pl.when(z > 0)
+    def _():
+        place(0)
+        make_names()
 
     def step(k):
-        merge(k)
-        if k + 1 < steps:
-            place(k + 1)
+        @pl.when(z > 0)
+        def _():
+            merge(k)
+            if k + 1 < steps:
+                place(k + 1)
 
     if square:
-        named = False
         for kind, at, *rest in timetable(sizes, blocks):
             if kind == "merge":
                 step(at)
@@ -570,9 +583,6 @@
             elif kind == "done":
                 complete(at)
             else:
-                if not named:
-                    pl.when(z == 0)(make_names)
-                    named = True
                 spans, final = rest
                 attend(at, [(spot ^ o, start, size) for o, start, size in spans])
                 if final:
@@ -585,8 +595,6 @@
             at = k - PASS_LAG
             if at < 0:
                 continue
-            if at == 0:
-                pl.when(z == 0)(make_names)
             pass_on(at)
 
             @pl.loop(0, blocks * parts)

time: 51.7 us -> 50 us (0.967)
  Pallas kernels: 49.5 us -> 47.8 us
    pallas_call x1, Pallas kernels: 49.5 us -> 47.8 us  [local(): pl.pallas_call(functools.partial(fused_kernel, shards, sizes), out_shape=...]
where the time goes in v4:
time: 50 us; the launch traced here: 49.8 us
  Pallas kernels  47.8 us (96%)
  local copies, waits for them, and re-layouts  1.32 us (3%)
  between operations  0.66 us (1%)
    pallas_call x1, Pallas kernels, local(): pl.pallas_call(functools.partial(fused_kernel, shards, sizes), out_shape=...  47.8 us
    unnamed x1, local copies, waits for them, and re-layouts  1.32 us

profile of v4, /device:TPU:24, one launch (start us, length us, event | category | flops | bytes accessed | tf_op | source)
XLA Modules:
  0.0 49.8 jit_solution(15399402422123395277)
XLA Ops:
  0.7 47.8 %fused.1 = bf16[512,2048]{1,0:T(8,128)(2,1)S(1)} custom-call(s32[1]{0:T(128)S(6)} %copy.9.count_ref, s32[4,128]{1,0:T(4,128)} %bitcast.2, f32[4,128]{1,0:T(4,128)} %bitcast.3, bf16[512,1024]{1,0:T(8,128)(2,1)} %q_ref.1, bf16[512,256]{1,0:T(8,128)(2,1)} %k_ref.1, bf16[512,256]{1,0:T(8,128)(2,1)} %v_ref.1, bf16[1024,4096]{1,0:T(8,128)(2,1)} %weight_ref.1), custom_call_target="tpu_custom_call" | custom-call | tf_op jit(solution)/shard_map/fused/pallas_call | solution.py:703
  48.5 1.3 %copy.10 = bf16[512,2048]{1,0:T(8,128)(2,1)} copy(bf16[512,2048]{1,0:T(8,128)(2,1)S(1)} %fused.1) | data formatting | bytes 4194304

commit v5 on v4

--- a/solution.py
+++ b/solution.py
@@ -27,6 +27,7 @@
 UNIT_COST = 0.2
 KEY_COST = 0.0016
 PASS_LAG = 3
+ROUTED = 1
 SPARE = 10 << 20
 FAR = 1 << 28
 LOW = -1e30
@@ -80,6 +81,8 @@
     while sum(sizes) < room:
         grown = TILE << len(sizes) if plane == SPAN else step
         sizes.append(min(grown, step, room - sum(sizes)))
+    if sizes[-1] > 2 * TILE:
+        sizes[-1:] = [sizes[-1] - TILE, TILE]
     return tuple(sizes)
 
 
@@ -116,15 +119,19 @@
         if merged < steps and merge_at[merged] <= now:
             events.append(("merge", merged))
             now += MERGE_COST
-            link = max(link, now) + ROW_TIME * sizes[merged]
+            routed = merged >= steps - ROUTED
+            link = max(link, now) + ROW_TIME * sizes[merged] * (2 if routed else 1)
             pass_at[merged] = link + HOP_TIME
             found(0, merged)
             merged += 1
             continue
         if passed in pass_at and pass_at[passed] <= now:
             events.append(("pass", passed))
-            link = max(link, now) + ROW_TIME * sizes[passed] / 2
-            done_at[passed] = link + HOP_TIME
+            if passed < steps - ROUTED:
+                link = max(link, now) + ROW_TIME * sizes[passed] / 2
+                done_at[passed] = link + HOP_TIME
+            else:
+                done_at[passed] = pass_at[passed] + HOP_TIME / 3
             found(1, passed)
             found(2, passed)
             passed += 1
@@ -316,9 +323,6 @@
                 weight_ref.at[at, columns], got_w.at[at, :], swap_sem, (i,), {"head": other}
             )
         )
-    for c in swaps:
-        c.start()
-    loads[5].start()
 
     loads[3].wait()
 
@@ -433,6 +437,12 @@
         here = kv.at[spot ^ 3, inner(k), pl.ds(part * keyed, keyed)]
         return remote(here, here, relay_sem, (k, part), {"ctx": z * plane + (spot ^ 3)})
 
+    def relayed(k):
+        return square and k < steps - ROUTED
+
+    def sent_to(k):
+        return direct if relayed(k) or not square else (3,) + direct
+
     def merge(k):
         @pl.when(z > 0)
         def _():
@@ -443,20 +453,22 @@
         def _():
             up(k).start()
 
-        for o in direct:
+        for o in sent_to(k):
             across(k, o).start()
 
     def pass_on(k):
         for o in direct:
             across_in(k, o).wait_recv()
-        if square:
+        if relayed(k):
             for part, peer in ((0, 1), (1, 2)):
                 relay(k, part, peer).start()
 
     def complete(k):
-        if square:
+        if relayed(k):
             for part in range(2):
                 relay_in(k, part).wait_recv()
+        elif square:
+            across_in(k, 3).wait_recv()
 
     ranks = lines * pieces * plane
     lanes = -(-ranks // LANES) * LANES
@@ -578,6 +590,10 @@
         for kind, at, *rest in timetable(sizes, blocks):
             if kind == "merge":
                 step(at)
+                if at == 3:
+                    for c in swaps:
+                        c.start()
+                    loads[5].start()
             elif kind == "pass":
                 pass_on(at)
             elif kind == "done":
@@ -589,6 +605,9 @@
                     finish(at)
     else:
         parts = plane // SPAN
+        for c in swaps:
+            c.start()
+        loads[5].start()
         for k in range(steps + PASS_LAG):
             if k < steps:
                 step(k)
@@ -635,9 +654,9 @@
             c.wait_send()
     for k in range(steps):
         pl.when(z + 1 < lines)(lambda: up(k).wait_send())
-        for o in direct:
+        for o in sent_to(k):
             across(k, o).wait_send()
-        if square:
+        if relayed(k):
             for part, peer in ((0, 1), (1, 2)):
                 relay(k, part, peer).wait_send()
     for c in swaps:

time: 50 us -> 49.9 us (level)
  no operation moved by 1% of the time
where the time goes in v5:
time: 49.9 us; the launch traced here: 49.7 us
  Pallas kernels  47.7 us (96%)
  local copies, waits for them, and re-layouts  1.32 us (3%)
  between operations  0.66 us (1%)
    pallas_call x1, Pallas kernels, local(): pl.pallas_call(functools.partial(fused_kernel, shards, sizes), out_shape=...  47.7 us
    unnamed x1, local copies, waits for them, and re-layouts  1.32 us

profile of v5, /device:TPU:24, one launch (start us, length us, event | category | flops | bytes accessed | tf_op | source)
XLA Modules:
  0.0 49.7 jit_solution(553649085780179715)
XLA Ops:
  0.7 47.7 %fused.1 = bf16[512,2048]{1,0:T(8,128)(2,1)S(1)} custom-call(s32[1]{0:T(128)S(6)} %copy.9.count_ref, s32[4,128]{1,0:T(4,128)} %bitcast.2, f32[4,128]{1,0:T(4,128)} %bitcast.3, bf16[512,1024]{1,0:T(8,128)(2,1)} %q_ref.1, bf16[512,256]{1,0:T(8,128)(2,1)} %k_ref.1, bf16[512,256]{1,0:T(8,128)(2,1)} %v_ref.1, bf16[1024,4096]{1,0:T(8,128)(2,1)} %weight_ref.1), custom_call_target="tpu_custom_call" | custom-call | tf_op jit(solution)/shard_map/fused/pallas_call | solution.py:722
  48.4 1.3 %copy.10 = bf16[512,2048]{1,0:T(8,128)(2,1)} copy(bf16[512,2048]{1,0:T(8,128)(2,1)S(1)} %fused.1) | data formatting | bytes 4194304
